TPU v7x, 256 devices: a whole 4x4x8 slice. The times are simulated.
256 devices in a mesh: dp: 8 (over y, core), expert: 32 (over z, x).
Axes of the slice: x: 4, y: 4, z: 8, core: 2. Of those that a mesh axis runs over, the one named last changes fastest.
Arguments:
- route_experts: int32 [32768, 8], P(('dp', 'expert')), may hold values from 0 to 255, all different within a row; in each aligned block of 128 rows (0 to 127, 128 to 255, ...) at most 5 rows name the same one
- router_gate_weight: float32 [32768, 8], P(('dp', 'expert')), may hold values from 0.02 to 0.3
- forget_mask: int32 [32768], P(('dp', 'expert')), may hold values 0 or 1
- retain_mask: int32 [32768], P(('dp', 'expert')), may hold values 0 or 1
- layer_output: bfloat16 [32768, 3584], P(('dp', 'expert')), may hold values from -6 to 6
- frozen_output: bfloat16 [32768, 3584], P(('dp', 'expert')), may hold values from -6 to 6
- control_vector: float32 [3584], replicated, may hold values from 0.1 to 1
- saved_hidden: bfloat16 [2048, 160, 2048], P(('dp', 'expert')), may hold values from -6 to 6
- adapter_in: bfloat16 [2048, 16384], P('dp', 'expert'), may hold values from -0.125 to 0.125
- adapter_out: bfloat16 [3584, 16384], P('dp', 'expert'), may hold values from -0.09375 to 0.09375
Outputs:
- grad_in: float32 [2048, 16384], P('dp', 'expert')
- grad_out: float32 [3584, 16384], P('dp', 'expert')
Inputs may be any that keep to these rules, and one draw needn't show every extreme that they name: `route_experts`: each row names 8 different experts; within the 128 rows of one device no expert is named more than 5 times, a bound that some block reaches.
All inputs are finite; a program needn't handle non-finite values. No bound on the sum of `forget_mask` or of `retain_mask` on one device may be relied on, other than what follows from the above.
Results may differ from a plain program's by a relative error of at most 0.0041.
Values may be sent and summed in bfloat16 or wider, within the bound.
No kernel may reach another device: no remote copies, remote signals or barrier semaphores. Data moves between devices by JAX's collectives and lax.ppermute only.
A program may use at most 128 MiB of HBM per device.

v0:
```python
import functools

import jax
import jax.numpy as jnp
from jax import lax
from jax.experimental import pallas as pl
from jax.experimental.pallas import tpu as pltpu
from jax.sharding import Mesh
from jax.sharding import PartitionSpec as P


steer_coef = 20.0
retain_weight = 1.5
adapter_scale_factor = 2.0
grad_coef = 0.0625

CAP = 5
PADC = 8
VMEM_LIMIT = 58 * 1024 * 1024


def token_cotangent(layer_output, frozen_output, forget_mask, retain_mask, control_vector):
    unit = control_vector / jnp.sqrt(jnp.sum(control_vector * control_vector))
    current = layer_output.astype(jnp.float32)
    forget_term = current - steer_coef * unit[None, :]
    retain_term = current - frozen_output.astype(jnp.float32)
    forget_weight = forget_mask.astype(jnp.float32)[:, None]
    retain_part = retain_mask.astype(jnp.float32)[:, None]
    return grad_coef * (forget_weight * forget_term + retain_weight * retain_part * retain_term)


def slot_tables(route_experts, gate, experts_all):
    tokens = route_experts.shape[0]
    hit = route_experts[:, :, None] == jnp.arange(experts_all, dtype=jnp.int32)[None, None, :]
    named = jnp.any(hit, axis=1)
    weight = jnp.sum(jnp.where(hit, gate[:, :, None], 0.0), axis=1)
    row = lax.broadcasted_iota(jnp.int32, (tokens, tokens), 0)
    col = lax.broadcasted_iota(jnp.int32, (tokens, tokens), 1)
    before = (col < row).astype(jnp.bfloat16)
    rank = jnp.dot(before, named.astype(jnp.bfloat16), preferred_element_type=jnp.float32)
    slot = jnp.arange(CAP, dtype=jnp.float32)[:, None, None]
    taken = jnp.logical_and(named[None], rank[None] == slot)
    number = jnp.arange(1, tokens + 1, dtype=jnp.float32)[None, :, None]
    token = jnp.sum(jnp.where(taken, number, 0.0), axis=1) - 1.0
    weights = jnp.sum(jnp.where(taken, weight[None], 0.0), axis=1)
    return token, weights


def low_lanes(shape):
    return lax.broadcasted_iota(jnp.int32, shape, 1) < shape[1] // 2


def codes_kernel(hidden_ref, factor_ref, out_ref):
    factor = factor_ref[...]
    first = jnp.dot(hidden_ref[0], factor, preferred_element_type=jnp.float32)
    second = jnp.dot(hidden_ref[1], factor, preferred_element_type=jnp.float32)
    out_ref[...] = jnp.where(low_lanes(first.shape), first, second)


def codes_call(hidden, factor):
    experts, slots, width = hidden.shape
    columns = factor.shape[1]
    pair = 2 * columns // experts
    return pl.pallas_call(
        codes_kernel,
        grid=(experts // 2,),
        in_specs=[
            pl.BlockSpec((2, slots, width), lambda i: (i, 0, 0)),
            pl.BlockSpec((width, pair), lambda i: (0, i)),
        ],
        out_specs=pl.BlockSpec((slots, pair), lambda i: (0, i)),
        out_shape=jax.ShapeDtypeStruct((slots, columns), jnp.float32),
        cost_estimate=pl.CostEstimate(
            flops=2 * slots * width * columns * 2,
            bytes_accessed=2 * hidden.size + 2 * factor.size,
            transcendentals=0,
        ),
        name="codes",
    )(hidden, factor)


def grad_in_kernel(core_ref, hidden_ref, pick_ref, scale_ref, *refs):
    part_refs, (mine_ref, theirs_ref) = refs[:-2], refs[-2:]
    sums = []
    for part_ref in part_refs:
        total = part_ref[0]
        for n in range(1, part_ref.shape[0]):
            total = total + part_ref[n]
        sums.append(total)
    back = jnp.concatenate(sums, axis=0)
    lanes = back.shape[1]

    def split(value):
        high = value.astype(jnp.bfloat16)
        low = (value - high.astype(jnp.float32)).astype(jnp.bfloat16)
        return jnp.concatenate([high, low], axis=1)

    def join(value):
        return value[:, :lanes] + value[:, lanes:]

    back = join(jnp.dot(pick_ref[...], split(back), preferred_element_type=jnp.float32))
    both = split(back * scale_ref[...])
    dims = (((0,), (0,)), ((), ()))
    first = join(lax.dot_general(hidden_ref[0], both, dims, preferred_element_type=jnp.float32))
    second = join(lax.dot_general(hidden_ref[1], both, dims, preferred_element_type=jnp.float32))
    total = jnp.where(low_lanes(first.shape), first, second)
    others, width, _ = mine_ref.shape
    first_core = core_ref[0] == 0
    for y in range(others):
        one = total[2 * y * width : (2 * y + 1) * width]
        two = total[(2 * y + 1) * width : (2 * y + 2) * width]
        mine_ref[y] = jnp.where(first_core, one, two)
        theirs_ref[y] = jnp.where(first_core, two, one)


def grad_in_call(core, hidden, pick, scale, parts, others):
    experts, slots, width = hidden.shape
    columns = scale.shape[1]
    pair = 2 * columns // experts
    share = width // (2 * others)
    return pl.pallas_call(
        grad_in_kernel,
        grid=(experts // 2,),
        in_specs=[
            pl.BlockSpec(memory_space=pltpu.SMEM),
            pl.BlockSpec((2, slots, width), lambda i: (i, 0, 0)),
            pl.BlockSpec(pick.shape, lambda i: (0, 0)),
            pl.BlockSpec((slots, pair), lambda i: (0, i)),
        ]
        + [pl.BlockSpec(p.shape[:2] + (pair,), lambda i: (0, 0, i)) for p in parts],
        out_specs=[pl.BlockSpec((others, share, pair), lambda i: (0, 0, i))] * 2,
        out_shape=[jax.ShapeDtypeStruct((others, share, columns), jnp.float32)] * 2,
        cost_estimate=pl.CostEstimate(
            flops=4 * slots * width * columns * 2,
            bytes_accessed=2 * hidden.size + 4 * width * columns,
            transcendentals=0,
        ),
        name="grad_in",
    )(core, hidden, pick, scale, *parts)


def back_kernel(starts, index_ref, *refs):
    count = len(starts)
    token_refs, (factor_ref, back_ref, slot_ref) = refs[:count], (refs[count], *refs[-2:])
    rows = index_ref.shape[2]
    _, experts, slots, width = slot_ref.shape
    step = rows // experts
    depth = sum(t.shape[0] for t in token_refs) * step // slots
    lanes = 2 * (back_ref.shape[2] // experts)
    dims = (((0,), (0,)), ((), ()))
    position = lax.broadcasted_iota(jnp.int32, (depth, rows), 0)
    base = 0
    for first_pair, token_ref in zip(starts, token_refs):

        def dispatch(n, carry, token_ref=token_ref, base=base, first_pair=first_pair):
            chosen = index_ref[0, pl.ds(first_pair + n, 1), :]
            pick = (position == chosen).astype(jnp.float32).astype(jnp.bfloat16)
            source = token_ref[pl.ds(pl.multiple_of(n * depth, depth), depth), :]
            value = lax.dot_general(pick, source, dims, preferred_element_type=jnp.float32)
            value = value.astype(jnp.bfloat16)
            start = pl.multiple_of((base + n) * step, step)
            for e in range(experts):
                slot_ref[0, e, pl.ds(start, step), :] = value[e * step : (e + 1) * step]
            return carry

        pairs = token_ref.shape[0] // depth
        lax.fori_loop(0, pairs, dispatch, 0)
        base += pairs
    blocks, _, quarter, _ = factor_ref.shape
    for g in range(experts // 2):
        at = slice(g * lanes, (g + 1) * lanes)
        factor = factor_ref[:, 0, :, at].reshape(blocks * quarter, lanes)
        both = slot_ref[0, 2 * g : 2 * g + 2].reshape(2 * slots, width)
        result = jnp.dot(both, factor, preferred_element_type=jnp.float32)
        first, second = result[:slots], result[slots:]
        back_ref[0, :, at] = jnp.where(low_lanes(first.shape), first, second)


def back_call(index, tokens, starts, factor, experts, pair_depth, all_slots, before, into):
    groups, pairs, rows = index.shape
    width = tokens[0].shape[1]
    blocks, _, quarter, columns = factor.shape
    depth = sum(t.shape[0] for t in tokens)
    slots = depth // pair_depth * rows // experts
    more = [] if into is None else [into]
    return pl.pallas_call(
        functools.partial(back_kernel, tuple(starts)),
        grid=(groups,),
        in_specs=[pl.BlockSpec((1, pairs, rows), lambda i: (i, 0, 0))]
        + [pl.BlockSpec(t.shape, lambda i: (0, 0)) for t in tokens]
        + [pl.BlockSpec((blocks, 1, quarter, columns), lambda i: (0, i, 0, 0))]
        + [pl.BlockSpec(memory_space=pl.ANY)] * len(more),
        input_output_aliases={len(tokens) + 2: 0} if more else {},
        out_specs=[
            pl.BlockSpec((1, slots, columns), lambda i: (i, before // slots, 0)),
            pl.BlockSpec((1, experts, slots, width), lambda i: (i, 0, 0, 0)),
        ],
        out_shape=[
            jax.ShapeDtypeStruct((groups, all_slots, columns), jnp.float32),
            jax.ShapeDtypeStruct((groups, experts, slots, width), jnp.bfloat16),
        ],
        compiler_params=pltpu.CompilerParams(vmem_limit_bytes=VMEM_LIMIT),
        cost_estimate=pl.CostEstimate(
            flops=groups * 2 * (rows * depth * width + 4 * slots * width * columns),
            bytes_accessed=2 * depth * width + 2 * factor.size + 4 * slots * columns * groups
            + 2 * groups * experts * slots * width,
            transcendentals=0,
        ),
        name="back",
    )(index, *tokens, factor, *more)


def grad_out_kernel(core_ref, *refs):
    slot_refs, (codes_ref, mine_ref, theirs_ref) = refs[:-3], refs[-3:]
    dims = (((0,), (0,)), ((), ()))
    codes = codes_ref[0]
    first = jnp.concatenate([s[0, 0] for s in slot_refs], axis=0)
    second = jnp.concatenate([s[0, 1] for s in slot_refs], axis=0)
    first = lax.dot_general(first, codes, dims, preferred_element_type=jnp.float32)
    second = lax.dot_general(second, codes, dims, preferred_element_type=jnp.float32)
    grad = jnp.where(low_lanes(first.shape), first, second)
    others, _, quarter, _ = mine_ref.shape
    first_core = core_ref[0] == 0
    for y in range(others):
        one = grad[2 * y * quarter : (2 * y + 1) * quarter]
        two = grad[(2 * y + 1) * quarter : (2 * y + 2) * quarter]
        mine_ref[y, 0] = jnp.where(first_core, one, two)
        theirs_ref[y, 0] = jnp.where(first_core, two, one)


def grad_out_call(core, slot_parts, codes, others, quarter):
    groups, slots, columns = codes.shape
    _, experts, _, width = slot_parts[0].shape
    pair = 2 * columns // experts
    return pl.pallas_call(
        grad_out_kernel,
        grid=(groups, experts // 2),
        in_specs=[pl.BlockSpec(memory_space=pltpu.SMEM)]
        + [
            pl.BlockSpec((1, 2, s.shape[2], width), lambda i, g: (i, g, 0, 0)) for s in slot_parts
        ]
        + [pl.BlockSpec((1, slots, pair), lambda i, g: (i, 0, g))],
        out_specs=[pl.BlockSpec((others, 1, quarter, pair), lambda i, g: (0, i, 0, g))] * 2,
        out_shape=[jax.ShapeDtypeStruct((others, groups, quarter, columns), jnp.float32)] * 2,
        compiler_params=pltpu.CompilerParams(vmem_limit_bytes=VMEM_LIMIT),
        cost_estimate=pl.CostEstimate(
            flops=groups * 4 * slots * width * columns,
            bytes_accessed=2 * groups * experts * slots * width + 4 * groups * width * columns,
            transcendentals=0,
        ),
        name="grad_out",
    )(core, *slot_parts, codes)


def turn(blocks, shift):
    count = blocks.shape[0]
    return lax.dynamic_slice_in_dim(jnp.concatenate([blocks, blocks], axis=0), shift, count, 0)


def around(mine):
    size = lax.axis_size("z")
    up = [(i, (i + 1) % size) for i in range(size)]
    down = [(i, (i - 1) % size) for i in range(size)]
    half = mine.shape[0] // 2
    groups = [[(0, mine)]]
    low = high = mine
    for k in range(1, size // 2):
        low = lax.ppermute(low, "z", up)
        high = lax.ppermute(high, "z", down)
        found = [(2 * (size - k), low), (2 * k, high)]
        if k < size // 2 - 1:
            groups[0] += found
        else:
            groups.append(found)
    k = size // 2
    low = lax.ppermute(low[:half], "z", up)
    high = lax.ppermute(high[half:], "z", down)
    groups.append([(2 * k, low), (2 * k + 1, high)])
    return groups


def local(
    route_experts,
    router_gate_weight,
    forget_mask,
    retain_mask,
    layer_output,
    frozen_output,
    control_vector,
    saved_hidden,
    adapter_in,
    adapter_out,
):
    experts, slot_count, _ = saved_hidden.shape
    tokens, features = layer_output.shape
    columns = adapter_in.shape[1]
    rank = columns // experts
    zs, xs = lax.axis_size("z"), lax.axis_size("x")
    dps = lax.axis_size("y") * lax.axis_size("c")
    blocks = zs * xs
    quarter = features // (dps * xs)
    width = features // xs

    gathered_in = lax.all_gather(adapter_in, ("y", "c"), axis=0, tiled=True)

    cotangent = token_cotangent(
        layer_output, frozen_output, forget_mask, retain_mask, control_vector
    ).astype(jnp.bfloat16)
    parts = cotangent.reshape(tokens, dps, xs, quarter).transpose(2, 0, 1, 3)
    mine = lax.all_to_all(parts.reshape(xs * tokens, width), "x", 0, 0, tiled=True)
    groups = around(mine)

    token, weights = slot_tables(route_experts, router_gate_weight, blocks * experts)
    token = token.reshape(CAP, zs, 1, xs * experts).transpose(1, 2, 0, 3)
    token = jnp.broadcast_to(token, (zs, xs, CAP, xs * experts))
    weights = weights.reshape(CAP, zs, xs, experts).transpose(1, 2, 0, 3)
    table = jnp.concatenate([token, weights], axis=3)
    table = jnp.pad(
        table,
        ((0, 0), (0, 0), (0, PADC - CAP), (0, 128 - table.shape[3])),
        constant_values=-1.0,
    )
    table = lax.all_to_all(table.reshape(blocks * PADC, 128), ("z", "x"), 0, 0, tiled=True)
    table = table.reshape(blocks, PADC, 128)
    scale = table[:, :CAP, xs * experts : (xs + 1) * experts]
    scale = adapter_scale_factor * scale
    scale = jnp.broadcast_to(
        scale.reshape(slot_count, experts, 1), (slot_count, experts, rank)
    ).reshape(slot_count, columns)
    here = lax.axis_index("z")
    index = turn(table[:, :, : xs * experts].reshape(zs, xs, PADC, xs * experts), here)
    index = index.astype(jnp.int32)
    index = index.reshape(blocks // 2, 2, PADC, xs, experts)
    odd = jnp.arange(2, dtype=jnp.int32).reshape(1, 2, 1, 1, 1) * tokens
    index = jnp.where(index >= 0, index + odd, -1)
    index = index.transpose(3, 0, 4, 1, 2).reshape(xs, blocks // 2, experts * 2 * PADC)

    factor = lax.all_to_all(adapter_out, "x", 0, 0, tiled=True)
    factor = lax.all_gather(factor, ("y", "c"), axis=0, tiled=True)
    factor = factor.reshape(dps, xs, quarter, columns)

    order = [start // 2 for group in groups for start, _ in group]
    order = list(dict.fromkeys(order))
    slot = jnp.arange(slot_count, dtype=jnp.int32)
    ahead = lax.rem(slot // (xs * CAP) - here + zs, zs)
    place = sum(jnp.where(ahead == o, n, 0) for n, o in enumerate(order))
    place = (place * xs + lax.rem(slot // CAP, xs)) * PADC + lax.rem(slot, CAP)
    pick = place[:, None] == jnp.arange(blocks * PADC, dtype=jnp.int32)[None, :]
    pick = pick.astype(jnp.bfloat16)

    codes = codes_call(saved_hidden, gathered_in)
    codes = (lax.reduce_precision(codes, 8, 7) * scale).astype(jnp.bfloat16)
    codes = lax.dot_general(
        pick, codes, (((0,), (0,)), ((), ())), preferred_element_type=jnp.float32
    )
    codes = jnp.broadcast_to(codes.astype(jnp.bfloat16)[None], (xs, blocks * PADC, columns))
    codes = lax.all_to_all(codes, "x", 0, 0, tiled=True)

    step = 2 * PADC
    sizes = [sum(t.shape[0] for _, t in g) // (2 * tokens) * step for g in groups]
    places = [(sizes[0], 0), (sizes[1] + sizes[2], 0), (sizes[1] + sizes[2], sizes[1])]
    backs, slot_parts, part = [], [], None
    for n, group in enumerate(groups):
        starts, parts = [f[0] for f in group], [f[1] for f in group]
        into = part if places[n][1] else None
        part, slots = back_call(index, parts, starts, factor, experts, 2 * tokens, *places[n], into)
        slot_parts.append(slots)
        if n != 1:
            backs.append(lax.all_to_all(part, "x", 0, 0, tiled=True))
    others = lax.axis_size("y")
    core = lax.axis_index("c").astype(jnp.int32).reshape(1)
    twins = [(0, 1), (1, 0)]
    out_mine, out_theirs = grad_out_call(core, slot_parts, codes, others, quarter)
    out_theirs = lax.ppermute(out_theirs, "c", twins)
    in_mine, in_theirs = grad_in_call(core, saved_hidden, pick, scale, backs, others)
    in_theirs = lax.ppermute(in_theirs, "c", twins)
    grad_out = (out_mine + out_theirs).astype(jnp.bfloat16)
    grad_out = grad_out.reshape(others * xs, quarter, columns)
    grad_out = lax.all_to_all(grad_out, ("y", "x"), 0, 0, tiled=True)
    grad_out = grad_out.reshape(others, xs * quarter, columns)
    grad_out = jnp.sum(grad_out.astype(jnp.float32), axis=0)
    grad_in = (in_mine + in_theirs).astype(jnp.bfloat16)
    grad_in = lax.all_to_all(grad_in, "y", 0, 0, tiled=True)
    grad_in = jnp.sum(grad_in.astype(jnp.float32), axis=0)
    return (grad_in, grad_out)


def solution(mesh):
    dps, blocks = mesh.devices.shape
    xs = 4 if blocks >= 32 else 2
    cores = 2
    fine = Mesh(
        mesh.devices.reshape(dps // cores, cores, blocks // xs, xs), ("y", "c", "z", "x")
    )
    dp, ep = ("y", "c"), ("z", "x")
    return jax.shard_map(
        local,
        mesh=fine,
        in_specs=(
            P(dp + ep, None),
            P(dp + ep, None),
            P(dp + ep),
            P(dp + ep),
            P(dp + ep, None),
            P(dp + ep, None),
            P(),
            P(dp + ep, None, None),
            P(dp, ep),
            P(dp, ep),
        ),
        out_specs=(P(dp, ep), P(dp, ep)),
        check_vma=False,
    )
```

profile of v0, /device:TPU:1, one launch (start us, length us, event | category | flops | bytes accessed | tf_op | source)
XLA Modules:
  0.0 248.5 jit_solution(14720572574599641770)
XLA Ops:
  7.2 0.7 all-gather.5.cloned.1.call-update
  8.0 11.5 %all_to_all.57 = bf16[4,112,512]{2,1,0:T(8,128)(2,1)} all-to-all(bf16[4,112,512]{2,1,0:T(8,128)(2,1)} %bitcast.40), channel_id=1, replica_groups=mesh['y'=4,'c'=2,'z'=8,'x'=4] {'x'}, dimensions={0} | all-to-all | bytes 917504 | tf_op jit(solution)/shard_map/all_to_all | solution.py:338
  19.5 0.6 copy.66
  20.2 0.6 copy.67
  20.8 0.6 multiply_reduce_fusion
  22.2 1.6 fusion.3
  23.9 12.4 %all_to_all.58 = bf16[4,128,896]{1,2,0:T(8,128)(2,1)S(1)} all-to-all(bf16[4,128,896]{1,2,0:T(8,128)(2,1)S(1)} %bitcast.29), channel_id=1, replica_groups=mesh['y'=4,'c'=2,'z'=8,'x'=4] {'x'}, dimensions={0} | all-to-all | bytes 1835008 | tf_op jit(solution)/shard_map/all_to_all | solution.py:310
  36.2 0.6 copy.69
  36.8 5.5 %collective-permute-start = (bf16[512,896]{1,0:T(8,128)(2,1)S(1)}, bf16[512,896]{1,0:T(8,128)(2,1)S(1)}, u32[]{:S(2)}, u32[]{:S(2)}) collective-permute-start(bf16[512,896]{1,0:T(8,128)(2,1)S(1)} %bitcast.37), channel_id=1, source_target_pairs={{0,4},{4,8},{8,12},{12,16},{16,20},{20,24},{24,28},{28,0},{1,5},{5... | collective-permute-start | bytes 2752520 | tf_op jit(solution)/shard_map/ppermute | solution.py:268
  42.3 3.8 %collective-permute-start.1 = (bf16[512,896]{1,0:T(8,128)(2,1)S(1)}, bf16[512,896]{1,0:T(8,128)(2,1)}, u32[]{:S(2)}, u32[]{:S(2)}) collective-permute-start(bf16[512,896]{1,0:T(8,128)(2,1)S(1)} %bitcast.38), channel_id=1, source_target_pairs={{0,28},{4,0},{8,4},{12,8},{16,12},{20,16},{24,20},{28,24},{1,29},{... | collective-permute-start | bytes 2752520 | tf_op jit(solution)/shard_map/ppermute | solution.py:269
  46.2 0.4 fusion.5
  46.7 17.6 %collective-permute-done.refs_1_ = bf16[512,896]{1,0:T(8,128)(2,1)S(1)} collective-permute-done((bf16[512,896]{1,0:T(8,128)(2,1)S(1)}, bf16[512,896]{1,0:T(8,128)(2,1)S(1)}, u32[]{:S(2)}, u32[]{:S(2)}) %collective-permute-start) | collective-permute-done | bytes 917536 | tf_op jit(solution)/shard_map/ppermute | solution.py:268
  64.3 2.7 %collective-permute-start.3 = (bf16[512,896]{1,0:T(8,128)(2,1)}, bf16[512,896]{1,0:T(8,128)(2,1)}, u32[]{:S(2)}, u32[]{:S(2)}) collective-permute-start(bf16[512,896]{1,0:T(8,128)(2,1)} %collective-permute-done.1.refs_2_), channel_id=1, source_target_pairs={{0,28},{4,0},{8,4},{12,8},{16,12},{20,16},{24,20},{28,24},{1,29},{... | collective-permute-start | bytes 2752520 | tf_op jit(solution)/shard_map/ppermute | solution.py:269
  67.1 0.4 select_reduce_fusion
  68.2 0.7 pad.4.clone
  68.9 6.0 %all-to-all-start = ((f32[32,8,128]{2,1,0:T(8,128)}), f32[32,8,128]{2,1,0:T(8,128)S(1)}, u32[]{:S(2)}, u32[]{:S(2)}) async-start(f32[32,8,128]{2,1,0:T(8,128)} %bitcast.4), calls=%async_computation | async-start | bytes 262144 | tf_op jit(solution)/shard_map/all_to_all | solution.py:323
  74.9 9.7 %collective-permute-done.2.refs_3_ = bf16[512,896]{1,0:T(8,128)(2,1)} collective-permute-done((bf16[512,896]{1,0:T(8,128)(2,1)S(1)}, bf16[512,896]{1,0:T(8,128)(2,1)}, u32[]{:S(2)}, u32[]{:S(2)}) %collective-permute-start.2) | collective-permute-done | bytes 917536 | tf_op jit(solution)/shard_map/ppermute | solution.py:268
  84.6 3.1 %collective-permute-start.6 = (bf16[512,896]{1,0:T(8,128)(2,1)}, bf16[512,896]{1,0:T(8,128)(2,1)}, u32[]{:S(2)}, u32[]{:S(2)}) collective-permute-start(bf16[512,896]{1,0:T(8,128)(2,1)} %collective-permute-done.3.refs_4_), channel_id=1, source_target_pairs={{0,28},{4,0},{8,4},{12,8},{16,12},{20,16},{24,20},{28,24},{1,29},{... | collective-permute-start | bytes 2752520 | tf_op jit(solution)/shard_map/ppermute | solution.py:269
  88.6 5.4 %codes.1 = f32[160,512]{1,0:T(8,128)} custom-call(bf16[8,160,2048]{2,1,0:T(8,128)(2,1)} %hidden_ref.3, bf16[2048,512]{1,0:T(8,128)(2,1)} %all-gather.5.cloned.1.call-done.factor_ref), custom_call_target="tpu_custom_call" | custom-call | flops 671088640 | bytes 7340032 | tf_op jit(solution)/shard_map/codes/pallas_call | solution.py:64
  94.0 1.3 convolution_convert_fusion
  95.3 1.1 broadcast_in_dim.108
  96.4 3.5 %all-to-all-start.6 = ((bf16[4,256,512]{2,1,0:T(8,128)(2,1)}), bf16[4,256,512]{2,1,0:T(8,128)(2,1)S(1)}, u32[]{:S(2)}, u32[]{:S(2)}) async-start(bf16[4,256,512]{2,1,0:T(8,128)(2,1)} %broadcast_in_dim.108), calls=%async_computation.6 | async-start | bytes 2097152 | tf_op jit(solution)/shard_map/all_to_all | solution.py:357
  99.9 6.3 %collective-permute-done.4.refs_0_ = bf16[512,896]{1,0:T(8,128)(2,1)} collective-permute-done((bf16[512,896]{1,0:T(8,128)(2,1)}, bf16[512,896]{1,0:T(8,128)(2,1)}, u32[]{:S(2)}, u32[]{:S(2)}) %collective-permute-start.4) | collective-permute-done | bytes 917536 | tf_op jit(solution)/shard_map/ppermute | solution.py:268
  106.2 1.1 slice.18
  107.4 1.1 slice.19
  108.5 2.9 %collective-permute-start.7 = (bf16[256,896]{1,0:T(8,128)(2,1)S(1)}, bf16[256,896]{1,0:T(8,128)(2,1)}, u32[]{:S(2)}, u32[]{:S(2)}) collective-permute-start(bf16[256,896]{1,0:T(8,128)(2,1)S(1)} %slice.19), channel_id=1, source_target_pairs={{0,28},{4,0},{8,4},{12,8},{16,12},{20,16},{24,20},{28,24},{1,29},{... | collective-permute-start | bytes 1376264 | tf_op jit(solution)/shard_map/ppermute | solution.py:277
  111.9 0.4 copy.65
  112.3 0.7 copy.70.index_ref
  113.0 8.4 %back.4 = (f32[4,96,512]{2,1,0:T(8,128)}, bf16[4,8,64,896]{3,2,1,0:T(8,128)(2,1)}) custom-call(s32[4,16,128]{2,1,0:T(8,128)} %copy.70.index_ref, bf16[512,896]{1,0:T(8,128)(2,1)} %collective-permute-done.4.refs_0_, bf16[512,896]{1,0:T(8,128)(2,1)} %collective-permute-done.6.refs_1_, bf16[8,4,112,512]{3,2,1,0:T(8,128)(2,1)} %bitcast.31), custom_call_target="tpu_custom_call" | custom-call | flops 1879048192 | bytes 9699328 | tf_op jit(solution)/shard_map/back/pallas_call | solution.py:186
  121.4 0.7 copy-done.7
  122.2 5.2 %back.5 = (f32[4,96,512]{2,1,0:T(8,128)}, bf16[4,8,32,896]{3,2,1,0:T(8,128)(2,1)}) custom-call(s32[4,16,128]{2,1,0:T(8,128)} %copy.70.index_ref, bf16[256,896]{1,0:T(8,128)(2,1)} %copy-done.7, bf16[256,896]{1,0:T(8,128)(2,1)} %collective-permute-done.7.refs_1_, bf16[8,4,112,512]{3,2,1,0:T(8,128)(2,1)} %bitcast.32, ...), custom_call_target="tpu_custom_call", output_to_operand_aliasing={{0}: (4, {})} | custom-call | flops 939524096 | bytes 6684672 | tf_op jit(solution)/shard_map/back/pallas_call | solution.py:186
  127.4 3.5 %all-to-all-start.4 = ((f32[4,96,512]{2,1,0:T(8,128)}), f32[4,96,512]{2,1,0:T(8,128)S(1)}, u32[]{:S(2)}, u32[]{:S(2)}) async-start(f32[4,96,512]{2,1,0:T(8,128)} %get-tuple-element.14), calls=%async_computation.4 | async-start | bytes 1572864 | tf_op jit(solution)/shard_map/all_to_all | solution.py:369
  130.9 17.3 %back.3 = (f32[4,160,512]{2,1,0:T(8,128)}, bf16[4,8,160,896]{3,2,1,0:T(8,128)(2,1)}) custom-call(s32[4,16,128]{2,1,0:T(8,128)} %copy.70.index_ref, bf16[512,896]{1,0:T(8,128)(2,1)} %bitcast.39, bf16[512,896]{1,0:T(8,128)(2,1)} %copy-done.11, bf16[512,896]{1,0:T(8,128)(2,1)} %collective-permute-done.1.refs_2_, ...), custom_call_target="tpu_custom_call" | custom-call | flops 4697620480 | bytes 18743296 | tf_op jit(solution)/shard_map/back/pallas_call | solution.py:186
  148.2 4.2 %all-to-all-start.3 = ((f32[4,160,512]{2,1,0:T(8,128)}), f32[4,160,512]{2,1,0:T(8,128)S(1)}, u32[]{:S(2)}, u32[]{:S(2)}) async-start(f32[4,160,512]{2,1,0:T(8,128)} %get-tuple-element.12), calls=%async_computation.3 | async-start | bytes 2621440 | tf_op jit(solution)/shard_map/all_to_all | solution.py:369
  152.4 16.0 %grad_out.1 = (f32[4,4,112,512]{3,2,1,0:T(8,128)}, f32[4,4,112,512]{3,2,1,0:T(8,128)}) custom-call(s32[1]{0:T(128)} %bitcast.core_ref, bf16[4,8,160,896]{3,2,1,0:T(8,128)(2,1)} %get-tuple-element.17.refs_0_, bf16[4,8,64,896]{3,2,1,0:T(8,128)(2,1)} %get-tuple-element.18.refs_1_, bf16[4,8,32,896]{3,2,1,0:T(8,128)(2,1)} %get-tuple-element.19.refs_2_, ...), custom_call_target="tpu_custom_call" | custom-call | flops 1879048192 | bytes 22020096 | tf_op jit(solution)/shard_map/grad_out/pallas_call | solution.py:235
  168.4 5.8 %collective-permute-start.9 = (f32[4,4,112,512]{3,2,1,0:T(8,128)}, f32[4,4,112,512]{3,2,1,0:T(8,128)}, u32[]{:S(2)}, u32[]{:S(2)}) collective-permute-start(f32[4,4,112,512]{3,2,1,0:T(8,128)} %get-tuple-element.21), channel_id=1, source_target_pairs={{0,32},{32,0},{1,33},{33,1},{2,34},{34,2},{3,35},{35,3},{4,36},{36... | collective-permute-start | bytes 11010056 | tf_op jit(solution)/shard_map/ppermute | solution.py:374
  174.2 0.7 fusion.7.pick_ref
  175.0 1.1 copy-done
  176.0 7.8 %grad_in.1 = (f32[4,256,512]{2,1,0:T(8,128)}, f32[4,256,512]{2,1,0:T(8,128)}) custom-call(s32[1]{0:T(128)} %bitcast.core_ref, bf16[8,160,2048]{2,1,0:T(8,128)(2,1)} %hidden_ref.3, bf16[160,256]{1,0:T(8,128)(2,1)} %fusion.7.pick_ref, f32[160,512]{1,0:T(8,128)} %copy-done.3, f32[4,160,512]{2,1,0:T(8,128)} %copy-done, f32[4,96,512]{2,1,0:T(8,128)} %copy-done.2), custom_call_target="tpu_custom_call" | custom-call | flops 1342177280 | bytes 9437184 | tf_op jit(solution)/shard_map/grad_in/pallas_call | solution.py:121
  183.9 4.4 %collective-permute-done.8 = f32[4,256,512]{2,1,0:T(8,128)S(1)} collective-permute-done((f32[4,256,512]{2,1,0:T(8,128)}, f32[4,256,512]{2,1,0:T(8,128)S(1)}, u32[]{:S(2)}, u32[]{:S(2)}) %collective-permute-start.8) | collective-permute-done | bytes 2097184 | tf_op jit(solution)/shard_map/ppermute | solution.py:376
  188.2 2.9 %add_convert_fusion.1 = bf16[4,256,512]{2,1,0:T(8,128)(2,1)} fusion(f32[4,256,512]{2,1,0:T(8,128)} %get-tuple-element.15, f32[4,256,512]{2,1,0:T(8,128)S(1)} %collective-permute-done.8), kind=kLoop, calls=%fused_computation.5 | loop fusion | flops 1048576 | bytes 5242880 | tf_op jit(solution)/shard_map/convert_element_type | solution.py:382
  191.1 4.3 %all-to-all-start.5 = ((bf16[4,256,512]{2,1,0:T(8,128)(2,1)}), bf16[4,256,512]{2,1,0:T(8,128)(2,1)S(1)}, u32[]{:S(2)}, u32[]{:S(2)}) async-start(bf16[4,256,512]{2,1,0:T(8,128)(2,1)} %add_convert_fusion.1), calls=%async_computation.5 | async-start | bytes 2097152 | tf_op jit(solution)/shard_map/all_to_all | solution.py:383
  195.4 5.2 %add_convert_fusion = bf16[4,4,112,512]{3,2,1,0:T(8,128)(2,1)} fusion(f32[4,4,112,512]{3,2,1,0:T(8,128)} %get-tuple-element.20, f32[4,4,112,512]{3,2,1,0:T(8,128)} %collective-permute-done.9), kind=kLoop, calls=%fused_computation.1 | loop fusion | flops 1835008 | bytes 9175040 | tf_op jit(solution)/shard_map/convert_element_type | solution.py:377
  200.6 9.6 %all-to-all-done.5 = bf16[4,256,512]{2,1,0:T(8,128)(2,1)S(1)} async-done(((bf16[4,256,512]{2,1,0:T(8,128)(2,1)}), bf16[4,256,512]{2,1,0:T(8,128)(2,1)S(1)}, u32[]{:S(2)}, u32[]{:S(2)}) %all-to-all-start.5) | async-done | bytes 1048608 | tf_op jit(solution)/shard_map/all_to_all | solution.py:383
  210.2 5.2 %all-to-all-start.7 = ((bf16[16,112,512]{2,1,0:T(8,128)(2,1)}), bf16[16,112,512]{2,1,0:T(8,128)(2,1)S(1)}, u32[]{:S(2)}, u32[]{:S(2)}) async-start(bf16[16,112,512]{2,1,0:T(8,128)(2,1)} %bitcast.28), calls=%async_computation.7 | async-start | bytes 3670016 | tf_op jit(solution)/shard_map/all_to_all | solution.py:379
  215.4 0.9 convert_reduce_fusion.1
  216.4 24.1 %all-to-all-done.7 = bf16[16,112,512]{2,1,0:T(8,128)(2,1)S(1)} async-done(((bf16[16,112,512]{2,1,0:T(8,128)(2,1)}), bf16[16,112,512]{2,1,0:T(8,128)(2,1)S(1)}, u32[]{:S(2)}, u32[]{:S(2)}) %all-to-all-start.7) | async-done | bytes 1835040 | tf_op jit(solution)/shard_map/all_to_all | solution.py:379
  240.4 1.2 convert_reduce_fusion
  (73 shorter events, 2.6 us)
Async XLA Ops:
  7.2 12.4 %copy-start.4 = (bf16[128,3584]{1,0:T(8,128)(2,1)S(1)}, bf16[128,3584]{1,0:T(8,128)(2,1)}, u32[]{:S(2)}) copy-start(bf16[128,3584]{1,0:T(8,128)(2,1)} %param.14) | copy-start | bytes 2752516
  7.2 13.0 %copy-start.5 = (bf16[128,3584]{1,0:T(8,128)(2,1)S(1)}, bf16[128,3584]{1,0:T(8,128)(2,1)}, u32[]{:S(2)}) copy-start(bf16[128,3584]{1,0:T(8,128)(2,1)} %param.15) | copy-start | bytes 2752516
  7.2 81.4 %all-gather.5.cloned.1.call-start = ((), (), s32[]{:S(2)}) async-start(), calls=%async_computation.9 | async-start | bytes 2359296 | tf_op jit(solution)/shard_map/all_gather | solution.py:304
  7.9 105.1 %all-gather.3.cloned.1.call-start = ((), (), s32[]{:S(2)}) async-start(), calls=%async_computation.8 | async-start | bytes 4128768 | tf_op jit(solution)/shard_map/all_gather | solution.py:339
  19.5 1.3 copy-start.8
  19.5 2.6 %copy-start.12 = (s32[128]{0:T(128)S(1)}, s32[128]{0:T(128)}, u32[]{:S(2)}) copy-start(s32[128]{0:T(128)} %param.12) | copy-start | bytes 1540
  19.5 2.6 %copy-start.13 = (s32[128]{0:T(128)S(1)}, s32[128]{0:T(128)}, u32[]{:S(2)}) copy-start(s32[128]{0:T(128)} %param.13) | copy-start | bytes 1540
  23.8 22.3 %copy-start.9 = (s32[128,8]{0,1:T(8,128)S(1)}, s32[128,8]{0,1:T(8,128)}, u32[]{:S(2)}) copy-start(s32[128,8]{0,1:T(8,128)} %param.10) | copy-start | bytes 12292
  23.8 43.1 %copy-start.10 = (f32[128,8]{0,1:T(8,128)S(1)}, f32[128,8]{0,1:T(8,128)}, u32[]{:S(2)}) copy-start(f32[128,8]{0,1:T(8,128)} %param.11) | copy-start | bytes 12292
  36.8 51.8 %copy-start.6 = (bf16[4,128,896]{2,1,0:T(8,128)(2,1)}, bf16[4,128,896]{2,1,0:T(8,128)(2,1)S(1)}, u32[]{:S(2)}) copy-start(bf16[4,128,896]{2,1,0:T(8,128)(2,1)S(1)} %copy.69) | copy-start | bytes 2752516
  36.8 27.5 %collective-permute-start = (bf16[512,896]{1,0:T(8,128)(2,1)S(1)}, bf16[512,896]{1,0:T(8,128)(2,1)S(1)}, u32[]{:S(2)}, u32[]{:S(2)}) collective-permute-start(bf16[512,896]{1,0:T(8,128)(2,1)S(1)} %bitcast.37), channel_id=1, source_target_pairs={{0,4},{4,8},{8,12},{12,16},{16,20},{20,24},{24,28},{28,0},{1,5},{5... | collective-permute-start | bytes 2752520 | tf_op jit(solution)/shard_map/ppermute | solution.py:268
  42.3 22.0 %collective-permute-start.1 = (bf16[512,896]{1,0:T(8,128)(2,1)S(1)}, bf16[512,896]{1,0:T(8,128)(2,1)}, u32[]{:S(2)}, u32[]{:S(2)}) collective-permute-start(bf16[512,896]{1,0:T(8,128)(2,1)S(1)} %bitcast.38), channel_id=1, source_target_pairs={{0,28},{4,0},{8,4},{12,8},{16,12},{20,16},{24,20},{28,24},{1,29},{... | collective-permute-start | bytes 2752520 | tf_op jit(solution)/shard_map/ppermute | solution.py:269
  64.3 23.5 %copy-start.11 = (bf16[512,896]{1,0:T(8,128)(2,1)}, bf16[512,896]{1,0:T(8,128)(2,1)S(1)}, u32[]{:S(2)}) copy-start(bf16[512,896]{1,0:T(8,128)(2,1)S(1)} %collective-permute-done.refs_1_) | copy-start | bytes 2752516
  64.3 20.3 %collective-permute-start.2 = (bf16[512,896]{1,0:T(8,128)(2,1)S(1)}, bf16[512,896]{1,0:T(8,128)(2,1)}, u32[]{:S(2)}, u32[]{:S(2)}) collective-permute-start(bf16[512,896]{1,0:T(8,128)(2,1)S(1)} %collective-permute-done.refs_1_), channel_id=1, source_target_pairs={{0,4},{4,8},{8,12},{12,16},{16,20},{20,24},{24,28},{28,0},{1,5},{5... | collective-permute-start | bytes 2752520 | tf_op jit(solution)/shard_map/ppermute | solution.py:268
  64.3 20.3 %collective-permute-start.3 = (bf16[512,896]{1,0:T(8,128)(2,1)}, bf16[512,896]{1,0:T(8,128)(2,1)}, u32[]{:S(2)}, u32[]{:S(2)}) collective-permute-start(bf16[512,896]{1,0:T(8,128)(2,1)} %collective-permute-done.1.refs_2_), channel_id=1, source_target_pairs={{0,28},{4,0},{8,4},{12,8},{16,12},{20,16},{24,20},{28,24},{1,29},{... | collective-permute-start | bytes 2752520 | tf_op jit(solution)/shard_map/ppermute | solution.py:269
  68.9 18.9 %all-to-all-start = ((f32[32,8,128]{2,1,0:T(8,128)}), f32[32,8,128]{2,1,0:T(8,128)S(1)}, u32[]{:S(2)}, u32[]{:S(2)}) async-start(f32[32,8,128]{2,1,0:T(8,128)} %bitcast.4), calls=%async_computation | async-start | bytes 262144 | tf_op jit(solution)/shard_map/all_to_all | solution.py:323
  84.6 21.6 %collective-permute-start.4 = (bf16[512,896]{1,0:T(8,128)(2,1)}, bf16[512,896]{1,0:T(8,128)(2,1)}, u32[]{:S(2)}, u32[]{:S(2)}) collective-permute-start(bf16[512,896]{1,0:T(8,128)(2,1)} %collective-permute-done.2.refs_3_), channel_id=1, source_target_pairs={{0,4},{4,8},{8,12},{12,16},{16,20},{20,24},{24,28},{28,0},{1,5},{5... | collective-permute-start | bytes 2752520 | tf_op jit(solution)/shard_map/ppermute | solution.py:268
  84.6 22.8 %collective-permute-start.6 = (bf16[512,896]{1,0:T(8,128)(2,1)}, bf16[512,896]{1,0:T(8,128)(2,1)}, u32[]{:S(2)}, u32[]{:S(2)}) collective-permute-start(bf16[512,896]{1,0:T(8,128)(2,1)} %collective-permute-done.3.refs_4_), channel_id=1, source_target_pairs={{0,28},{4,0},{8,4},{12,8},{16,12},{20,16},{24,20},{28,24},{1,29},{... | collective-permute-start | bytes 2752520 | tf_op jit(solution)/shard_map/ppermute | solution.py:269
  88.6 5.4 %copy-start.3 = (f32[160,512]{1,0:T(8,128)}, f32[160,512]{1,0:T(8,128)S(1)}, u32[]{:S(2)}) copy-start(f32[160,512]{1,0:T(8,128)S(1)} %reshape.143.scale_ref) | copy-start | bytes 983044
  96.4 31.0 %all-to-all-start.6 = ((bf16[4,256,512]{2,1,0:T(8,128)(2,1)}), bf16[4,256,512]{2,1,0:T(8,128)(2,1)S(1)}, u32[]{:S(2)}, u32[]{:S(2)}) async-start(bf16[4,256,512]{2,1,0:T(8,128)(2,1)} %broadcast_in_dim.108), calls=%async_computation.6 | async-start | bytes 2097152 | tf_op jit(solution)/shard_map/all_to_all | solution.py:357
  107.3 14.1 %collective-permute-start.5 = (bf16[256,896]{1,0:T(8,128)(2,1)S(1)}, bf16[256,896]{1,0:T(8,128)(2,1)S(1)}, u32[]{:S(2)}, u32[]{:S(2)}) collective-permute-start(bf16[256,896]{1,0:T(8,128)(2,1)S(1)} %slice.18), channel_id=1, source_target_pairs={{0,4},{4,8},{8,12},{12,16},{16,20},{20,24},{24,28},{28,0},{1,5},{5... | collective-permute-start | bytes 1376264 | tf_op jit(solution)/shard_map/ppermute | solution.py:276
  108.5 12.9 %collective-permute-start.7 = (bf16[256,896]{1,0:T(8,128)(2,1)S(1)}, bf16[256,896]{1,0:T(8,128)(2,1)}, u32[]{:S(2)}, u32[]{:S(2)}) collective-permute-start(bf16[256,896]{1,0:T(8,128)(2,1)S(1)} %slice.19), channel_id=1, source_target_pairs={{0,28},{4,0},{8,4},{12,8},{16,12},{20,16},{24,20},{28,24},{1,29},{... | collective-permute-start | bytes 1376264 | tf_op jit(solution)/shard_map/ppermute | solution.py:277
  121.4 0.8 copy-start.7
  127.3 20.9 %copy-start.1 = (bf16[4,256,512]{2,1,0:T(8,128)(2,1)}, bf16[4,256,512]{2,1,0:T(8,128)(2,1)S(1)}, u32[]{:S(2)}) copy-start(bf16[4,256,512]{2,1,0:T(8,128)(2,1)S(1)} %all-to-all-done.6.refs_3_) | copy-start | bytes 3145732
  127.4 20.9 %all-to-all-start.4 = ((f32[4,96,512]{2,1,0:T(8,128)}), f32[4,96,512]{2,1,0:T(8,128)S(1)}, u32[]{:S(2)}, u32[]{:S(2)}) async-start(f32[4,96,512]{2,1,0:T(8,128)} %get-tuple-element.14), calls=%async_computation.4 | async-start | bytes 1572864 | tf_op jit(solution)/shard_map/all_to_all | solution.py:369
  148.2 20.2 %copy-start.2 = (f32[4,96,512]{2,1,0:T(8,128)}, f32[4,96,512]{2,1,0:T(8,128)S(1)}, u32[]{:S(2)}) copy-start(f32[4,96,512]{2,1,0:T(8,128)S(1)} %all-to-all-done.4.refs_1_) | copy-start | bytes 2359300
  148.2 26.7 %all-to-all-start.3 = ((f32[4,160,512]{2,1,0:T(8,128)}), f32[4,160,512]{2,1,0:T(8,128)S(1)}, u32[]{:S(2)}, u32[]{:S(2)}) async-start(f32[4,160,512]{2,1,0:T(8,128)} %get-tuple-element.12), calls=%async_computation.3 | async-start | bytes 2621440 | tf_op jit(solution)/shard_map/all_to_all | solution.py:369
  168.4 27.0 %collective-permute-start.9 = (f32[4,4,112,512]{3,2,1,0:T(8,128)}, f32[4,4,112,512]{3,2,1,0:T(8,128)}, u32[]{:S(2)}, u32[]{:S(2)}) collective-permute-start(f32[4,4,112,512]{3,2,1,0:T(8,128)} %get-tuple-element.21), channel_id=1, source_target_pairs={{0,32},{32,0},{1,33},{33,1},{2,34},{34,2},{3,35},{35,3},{4,36},{36... | collective-permute-start | bytes 11010056 | tf_op jit(solution)/shard_map/ppermute | solution.py:374
  175.0 1.1 copy-start
  183.8 4.4 %collective-permute-start.8 = (f32[4,256,512]{2,1,0:T(8,128)}, f32[4,256,512]{2,1,0:T(8,128)S(1)}, u32[]{:S(2)}, u32[]{:S(2)}) collective-permute-start(f32[4,256,512]{2,1,0:T(8,128)} %get-tuple-element.16), channel_id=1, source_target_pairs={{0,32},{32,0},{1,33},{33,1},{2,34},{34,2},{3,35},{35,3},{4,36},{36... | collective-permute-start | bytes 6291464 | tf_op jit(solution)/shard_map/ppermute | solution.py:376
  191.1 19.1 %all-to-all-start.5 = ((bf16[4,256,512]{2,1,0:T(8,128)(2,1)}), bf16[4,256,512]{2,1,0:T(8,128)(2,1)S(1)}, u32[]{:S(2)}, u32[]{:S(2)}) async-start(bf16[4,256,512]{2,1,0:T(8,128)(2,1)} %add_convert_fusion.1), calls=%async_computation.5 | async-start | bytes 2097152 | tf_op jit(solution)/shard_map/all_to_all | solution.py:383
  210.2 30.2 %all-to-all-start.7 = ((bf16[16,112,512]{2,1,0:T(8,128)(2,1)}), bf16[16,112,512]{2,1,0:T(8,128)(2,1)S(1)}, u32[]{:S(2)}, u32[]{:S(2)}) async-start(bf16[16,112,512]{2,1,0:T(8,128)(2,1)} %bitcast.28), calls=%async_computation.7 | async-start | bytes 3670016 | tf_op jit(solution)/shard_map/all_to_all | solution.py:379
Sparse Core Ops, SparseCore 0:
  9.9 32.0 all-gather.4
  43.8 32.8 all-gather.2
where the time goes:
time: 250 us; the launch traced here: 248 us
  waiting for transfers between devices  72.5 us (29%)
  Pallas kernels  60.1 us (24%)
  starting transfers between devices  50.7 us (20%)
  blocking collectives  23.9 us (10%)
  between operations  15.2 us (6%)
  other arithmetic  14.5 us (6%)
  local copies, waits for them, and re-layouts  10.2 us (4%)
    ppermute x3, waiting for transfers between devices, around(): low = lax.ppermute(low, 'z', up)  33.7 us
    pallas_call x3, Pallas kernels, back_call(): pl.pallas_call(functools.partial(back_kernel, tuple(starts)), grid=(group...  30.9 us
    all_to_all x1, waiting for transfers between devices, local(): grad_out = lax.all_to_all(grad_out, ('y', 'x'), 0, 0, tiled=True)  24.1 us
    pallas_call x1, Pallas kernels, grad_out_call(): pl.pallas_call(grad_out_kernel, grid=(groups, experts // 2), in_specs=[pl...  16 us
    all_to_all x1, blocking collectives, local(): lax.all_to_all(parts.reshape(xs * tokens, width), 'x', 0, 0, tiled=True)  12.4 us
    all_to_all x1, blocking collectives, local(): factor = lax.all_to_all(adapter_out, 'x', 0, 0, tiled=True)  11.5 us
    ppermute x3, starting transfers between devices, around(): high = lax.ppermute(high, 'z', down)  9.63 us
    all_to_all x1, waiting for transfers between devices, local(): grad_in = lax.all_to_all(grad_in, 'y', 0, 0, tiled=True)  9.62 us
  transfers between devices with their start and end apart: 18, of which 6 were waited for; matrix products, arithmetic and copies ran while one was open for 9% of the time, Pallas kernels for 24%

commit v1 on v0

--- a/solution.py
+++ b/solution.py
@@ -50,33 +50,47 @@
     return lax.broadcasted_iota(jnp.int32, shape, 1) < shape[1] // 2
 
 
-def codes_kernel(hidden_ref, factor_ref, out_ref):
-    factor = factor_ref[...]
+def own_order(here_ref, mine, theirs, others):
+    first_core = here_ref[0] == 0
+    parts = []
+    for y in range(others):
+        at = lax.rem(y - here_ref[1] + others, others)
+        one, two = mine(at), theirs(at)
+        parts += [jnp.where(first_core, one, two), jnp.where(first_core, two, one)]
+    return jnp.concatenate(parts, axis=0)
+
+
+def codes_kernel(here_ref, hidden_ref, mine_ref, theirs_ref, out_ref):
+    factor = own_order(
+        here_ref, lambda at: mine_ref[at], lambda at: theirs_ref[at], mine_ref.shape[0]
+    )
     first = jnp.dot(hidden_ref[0], factor, preferred_element_type=jnp.float32)
     second = jnp.dot(hidden_ref[1], factor, preferred_element_type=jnp.float32)
     out_ref[...] = jnp.where(low_lanes(first.shape), first, second)
 
 
-def codes_call(hidden, factor):
+def codes_call(here, hidden, mine, theirs):
     experts, slots, width = hidden.shape
-    columns = factor.shape[1]
+    others, share, columns = mine.shape
     pair = 2 * columns // experts
     return pl.pallas_call(
         codes_kernel,
         grid=(experts // 2,),
         in_specs=[
+            pl.BlockSpec(memory_space=pltpu.SMEM),
             pl.BlockSpec((2, slots, width), lambda i: (i, 0, 0)),
-            pl.BlockSpec((width, pair), lambda i: (0, i)),
+            pl.BlockSpec((others, share, pair), lambda i: (0, 0, i)),
+            pl.BlockSpec((others, share, pair), lambda i: (0, 0, i)),
         ],
         out_specs=pl.BlockSpec((slots, pair), lambda i: (0, i)),
         out_shape=jax.ShapeDtypeStruct((slots, columns), jnp.float32),
         cost_estimate=pl.CostEstimate(
             flops=2 * slots * width * columns * 2,
-            bytes_accessed=2 * hidden.size + 2 * factor.size,
+            bytes_accessed=2 * hidden.size + 4 * mine.size,
             transcendentals=0,
         ),
         name="codes",
-    )(hidden, factor)
+    )(here, hidden, mine, theirs)
 
 
 def grad_in_kernel(core_ref, hidden_ref, pick_ref, scale_ref, *refs):
@@ -109,8 +123,9 @@
     for y in range(others):
         one = total[2 * y * width : (2 * y + 1) * width]
         two = total[(2 * y + 1) * width : (2 * y + 2) * width]
-        mine_ref[y] = jnp.where(first_core, one, two)
-        theirs_ref[y] = jnp.where(first_core, two, one)
+        at = lax.rem(y - core_ref[1] + others, others)
+        mine_ref[at] = jnp.where(first_core, one, two)
+        theirs_ref[at] = jnp.where(first_core, two, one)
 
 
 def grad_in_call(core, hidden, pick, scale, parts, others):
@@ -139,9 +154,10 @@
     )(core, hidden, pick, scale, *parts)
 
 
-def back_kernel(starts, index_ref, *refs):
+def back_kernel(starts, here_ref, index_ref, *refs):
     count = len(starts)
-    token_refs, (factor_ref, back_ref, slot_ref) = refs[:count], (refs[count], *refs[-2:])
+    token_refs, (mine_ref, theirs_ref) = refs[:count], refs[count : count + 2]
+    back_ref, slot_ref = refs[-2:]
     rows = index_ref.shape[2]
     _, experts, slots, width = slot_ref.shape
     step = rows // experts
@@ -166,31 +182,36 @@
         pairs = token_ref.shape[0] // depth
         lax.fori_loop(0, pairs, dispatch, 0)
         base += pairs
-    blocks, _, quarter, _ = factor_ref.shape
     for g in range(experts // 2):
         at = slice(g * lanes, (g + 1) * lanes)
-        factor = factor_ref[:, 0, :, at].reshape(blocks * quarter, lanes)
+        factor = own_order(
+            here_ref,
+            lambda n, at=at: mine_ref[n, 0, :, at],
+            lambda n, at=at: theirs_ref[n, 0, :, at],
+            mine_ref.shape[0],
+        )
         both = slot_ref[0, 2 * g : 2 * g + 2].reshape(2 * slots, width)
         result = jnp.dot(both, factor, preferred_element_type=jnp.float32)
         first, second = result[:slots], result[slots:]
         back_ref[0, :, at] = jnp.where(low_lanes(first.shape), first, second)
 
 
-def back_call(index, tokens, starts, factor, experts, pair_depth, all_slots, before, into):
+def back_call(here, index, tokens, starts, factor, experts, pair_depth, all_slots, before, into):
     groups, pairs, rows = index.shape
     width = tokens[0].shape[1]
-    blocks, _, quarter, columns = factor.shape
+    others, _, quarter, columns = factor[0].shape
     depth = sum(t.shape[0] for t in tokens)
     slots = depth // pair_depth * rows // experts
     more = [] if into is None else [into]
     return pl.pallas_call(
         functools.partial(back_kernel, tuple(starts)),
         grid=(groups,),
-        in_specs=[pl.BlockSpec((1, pairs, rows), lambda i: (i, 0, 0))]
+        in_specs=[pl.BlockSpec(memory_space=pltpu.SMEM)]
+        + [pl.BlockSpec((1, pairs, rows), lambda i: (i, 0, 0))]
         + [pl.BlockSpec(t.shape, lambda i: (0, 0)) for t in tokens]
-        + [pl.BlockSpec((blocks, 1, quarter, columns), lambda i: (0, i, 0, 0))]
+        + [pl.BlockSpec((others, 1, quarter, columns), lambda i: (0, i, 0, 0))] * 2
         + [pl.BlockSpec(memory_space=pl.ANY)] * len(more),
-        input_output_aliases={len(tokens) + 2: 0} if more else {},
+        input_output_aliases={len(tokens) + 4: 0} if more else {},
         out_specs=[
             pl.BlockSpec((1, slots, columns), lambda i: (i, before // slots, 0)),
             pl.BlockSpec((1, experts, slots, width), lambda i: (i, 0, 0, 0)),
@@ -202,12 +223,12 @@
         compiler_params=pltpu.CompilerParams(vmem_limit_bytes=VMEM_LIMIT),
         cost_estimate=pl.CostEstimate(
             flops=groups * 2 * (rows * depth * width + 4 * slots * width * columns),
-            bytes_accessed=2 * depth * width + 2 * factor.size + 4 * slots * columns * groups
+            bytes_accessed=2 * depth * width + 4 * factor[0].size + 4 * slots * columns * groups
             + 2 * groups * experts * slots * width,
             transcendentals=0,
         ),
         name="back",
-    )(index, *tokens, factor, *more)
+    )(here, index, *tokens, *factor, *more)
 
 
 def grad_out_kernel(core_ref, *refs):
@@ -257,6 +278,16 @@
     return lax.dynamic_slice_in_dim(jnp.concatenate([blocks, blocks], axis=0), shift, count, 0)
 
 
+def over_dp(part):
+    size = lax.axis_size("y")
+    stack = [part]
+    for k in range(1, size):
+        stack.append(lax.ppermute(part, "y", [((i + k) % size, i) for i in range(size)]))
+    mine = jnp.stack(stack)
+    theirs = lax.ppermute(mine, "c", [(0, 1), (1, 0)])
+    return mine, theirs
+
+
 def around(mine):
     size = lax.axis_size("z")
     up = [(i, (i + 1) % size) for i in range(size)]
@@ -301,7 +332,10 @@
     quarter = features // (dps * xs)
     width = features // xs
 
-    gathered_in = lax.all_gather(adapter_in, ("y", "c"), axis=0, tiled=True)
+    others = lax.axis_size("y")
+    twins = [(0, 1), (1, 0)]
+    where = jnp.stack([lax.axis_index("c"), lax.axis_index("y")]).astype(jnp.int32)
+    gathered_in = over_dp(adapter_in)
 
     cotangent = token_cotangent(
         layer_output, frozen_output, forget_mask, retain_mask, control_vector
@@ -336,8 +370,7 @@
     index = index.transpose(3, 0, 4, 1, 2).reshape(xs, blocks // 2, experts * 2 * PADC)
 
     factor = lax.all_to_all(adapter_out, "x", 0, 0, tiled=True)
-    factor = lax.all_gather(factor, ("y", "c"), axis=0, tiled=True)
-    factor = factor.reshape(dps, xs, quarter, columns)
+    factor = over_dp(factor.reshape(xs, quarter, columns))
 
     order = [start // 2 for group in groups for start, _ in group]
     order = list(dict.fromkeys(order))
@@ -348,7 +381,7 @@
     pick = place[:, None] == jnp.arange(blocks * PADC, dtype=jnp.int32)[None, :]
     pick = pick.astype(jnp.bfloat16)
 
-    codes = codes_call(saved_hidden, gathered_in)
+    codes = codes_call(where, saved_hidden, *gathered_in)
     codes = (lax.reduce_precision(codes, 8, 7) * scale).astype(jnp.bfloat16)
     codes = lax.dot_general(
         pick, codes, (((0,), (0,)), ((), ())), preferred_element_type=jnp.float32
@@ -363,25 +396,26 @@
     for n, group in enumerate(groups):
         starts, parts = [f[0] for f in group], [f[1] for f in group]
         into = part if places[n][1] else None
-        part, slots = back_call(index, parts, starts, factor, experts, 2 * tokens, *places[n], into)
+        part, slots = back_call(
+            where, index, parts, starts, factor, experts, 2 * tokens, *places[n], into
+        )
         slot_parts.append(slots)
         if n != 1:
             backs.append(lax.all_to_all(part, "x", 0, 0, tiled=True))
-    others = lax.axis_size("y")
-    core = lax.axis_index("c").astype(jnp.int32).reshape(1)
-    twins = [(0, 1), (1, 0)]
-    out_mine, out_theirs = grad_out_call(core, slot_parts, codes, others, quarter)
+    out_mine, out_theirs = grad_out_call(where, slot_parts, codes, others, quarter)
     out_theirs = lax.ppermute(out_theirs, "c", twins)
-    in_mine, in_theirs = grad_in_call(core, saved_hidden, pick, scale, backs, others)
+    in_mine, in_theirs = grad_in_call(where, saved_hidden, pick, scale, backs, others)
     in_theirs = lax.ppermute(in_theirs, "c", twins)
     grad_out = (out_mine + out_theirs).astype(jnp.bfloat16)
     grad_out = grad_out.reshape(others * xs, quarter, columns)
     grad_out = lax.all_to_all(grad_out, ("y", "x"), 0, 0, tiled=True)
     grad_out = grad_out.reshape(others, xs * quarter, columns)
     grad_out = jnp.sum(grad_out.astype(jnp.float32), axis=0)
-    grad_in = (in_mine + in_theirs).astype(jnp.bfloat16)
-    grad_in = lax.all_to_all(grad_in, "y", 0, 0, tiled=True)
-    grad_in = jnp.sum(grad_in.astype(jnp.float32), axis=0)
+    grad_in = in_mine[0] + in_theirs[0]
+    for k in range(1, others):
+        piece = (in_mine[k] + in_theirs[k]).astype(jnp.bfloat16)
+        piece = lax.ppermute(piece, "y", [(i, (i + k) % others) for i in range(others)])
+        grad_in = grad_in + piece.astype(jnp.float32)
     return (grad_in, grad_out)
 
 

time: 250 us -> 265 us (1.060)
  blocking collectives: 23.9 us -> 39.5 us
  between operations: 15.2 us -> 1.77 us
  starting transfers between devices: 50.7 us -> 60.1 us
  waiting for transfers between devices: 72.5 us -> 66.6 us
  local copies, waits for them, and re-layouts: 10.2 us -> 15.8 us
  other arithmetic: 14.5 us -> 17.7 us
    ppermute x0 -> x11, waiting for transfers between devices: none -> 48 us  [the longest x3 28.8 us: local(): lax.ppermute(piece, 'y', [(i, (i + k) % others) for i in range(others)])]
    ppermute x3, waiting for transfers between devices: 33.7 us -> 7.55 us  [around(): low = lax.ppermute(low, 'z', up)]
    all_to_all x1, waiting for transfers between devices: 24.1 us -> 0.01 us  [local(): grad_out = lax.all_to_all(grad_out, ('y', 'x'), 0, 0, tiled=True)]
    ppermute x0 -> x11, starting transfers between devices: none -> 13.8 us  [the longest x6 9.07 us: over_dp(): lax.ppermute(part, 'y', [((i + k) % size, i) for i in range(size)])]
    all_to_all x1, blocking collectives: 11.5 us -> 22.1 us  [local(): backs.append(lax.all_to_all(part, 'x', 0, 0, tiled=True))]
    all_to_all x2 -> x1, waiting for transfers between devices: 0.01 us -> 10.5 us  [local(): backs.append(lax.all_to_all(part, 'x', 0, 0, tiled=True))]
    all_to_all x1, waiting for transfers between devices: 9.62 us -> 0.2 us  [local(): factor = lax.all_to_all(adapter_out, 'x', 0, 0, tiled=True)]
    all_to_all x1, blocking collectives: 12.4 us -> 17.4 us  [local(): lax.all_to_all(parts.reshape(xs * tokens, width), 'x', 0, 0, tiled=True)]
  transfers between devices with their start and end apart: 18 -> 26, of which waited for: 6 -> 9; matrix products, arithmetic and copies ran while one was open for 9% -> 10% of each run, Pallas kernels for 24% -> 17%
where the time goes in v1:
time: 265 us; the launch traced here: 263 us
  waiting for transfers between devices  66.6 us (25%)
  Pallas kernels  60.5 us (23%)
  starting transfers between devices  60.1 us (23%)
  blocking collectives  39.5 us (15%)
  other arithmetic  17.7 us (7%)
  local copies, waits for them, and re-layouts  15.8 us (6%)
    pallas_call x3, Pallas kernels, back_call(): pl.pallas_call(functools.partial(back_kernel, tuple(starts)), grid=(group...  31.2 us
    ppermute x3, waiting for transfers between devices, local(): lax.ppermute(piece, 'y', [(i, (i + k) % others) for i in range(others)])  28.8 us
    all_to_all x1, blocking collectives, local(): backs.append(lax.all_to_all(part, 'x', 0, 0, tiled=True))  22.1 us
    ppermute x6, waiting for transfers between devices, over_dp(): lax.ppermute(part, 'y', [((i + k) % size, i) for i in range(size)])  19.3 us
    all_to_all x1, blocking collectives, local(): lax.all_to_all(parts.reshape(xs * tokens, width), 'x', 0, 0, tiled=True)  17.4 us
    pallas_call x1, Pallas kernels, grad_out_call(): pl.pallas_call(grad_out_kernel, grid=(groups, experts // 2), in_specs=[pl...  16.1 us
    ppermute x3, starting transfers between devices, around(): high = lax.ppermute(high, 'z', down)  11.6 us
    all_to_all x1, waiting for transfers between devices, local(): backs.append(lax.all_to_all(part, 'x', 0, 0, tiled=True))  10.5 us
  transfers between devices with their start and end apart: 26, of which 9 were waited for; matrix products, arithmetic and copies ran while one was open for 10% of the time, Pallas kernels for 17%

profile of v1, /device:TPU:1, one launch (start us, length us, event | category | flops | bytes accessed | tf_op | source)
XLA Modules:
  0.0 263.4 jit_solution(5508576287638233072)
XLA Ops:
  0.7 1.6 copy.66
  4.3 1.6 fusion.3
  6.0 17.4 %all_to_all.49 = bf16[4,128,896]{1,2,0:T(8,128)(2,1)S(1)} all-to-all(bf16[4,128,896]{1,2,0:T(8,128)(2,1)S(1)} %bitcast.50), channel_id=1, replica_groups=mesh['y'=4,'c'=2,'z'=8,'x'=4] {'x'}, dimensions={0} | all-to-all | bytes 1835008 | tf_op jit(solution)/shard_map/all_to_all | solution.py:344
  23.4 3.6 %all-to-all-start.2 = ((bf16[4,112,512]{2,1,0:T(8,128)(2,1)}), bf16[4,112,512]{2,1,0:T(8,128)(2,1)S(1)}, u32[]{:S(2)}, u32[]{:S(2)}) async-start(bf16[4,112,512]{2,1,0:T(8,128)(2,1)} %bitcast.13), calls=%async_computation.2 | async-start | bytes 917504 | tf_op jit(solution)/shard_map/all_to_all | solution.py:372
  27.6 1.7 collective-permute-start
  29.4 4.0 %collective-permute-start.1 = (bf16[512,896]{1,0:T(8,128)(2,1)S(1)}, bf16[512,896]{1,0:T(8,128)(2,1)}, u32[]{:S(2)}, u32[]{:S(2)}) collective-permute-start(bf16[512,896]{1,0:T(8,128)(2,1)S(1)} %bitcast.56), channel_id=1, source_target_pairs={{0,28},{4,0},{8,4},{12,8},{16,12},{20,16},{24,20},{28,24},{1,29},{... | collective-permute-start | bytes 2752520 | tf_op jit(solution)/shard_map/ppermute | solution.py:300
  33.7 1.4 collective-permute-start.6
  35.1 2.6 collective-permute-start.5
  37.7 1.1 collective-permute-start.4
  39.8 4.5 %collective-permute-done.6 = bf16[4,112,512]{2,1,0:T(8,128)(2,1)S(1)} collective-permute-done((bf16[4,112,512]{2,1,0:T(8,128)(2,1)S(1)}, bf16[4,112,512]{2,1,0:T(8,128)(2,1)S(1)}, u32[]{:S(2)}, u32[]{:S(2)}) %collective-permute-start.6) | collective-permute-done | bytes 458784 | tf_op jit(solution)/shard_map/ppermute | solution.py:285
  44.4 10.8 %collective-permute-done.5 = bf16[4,112,512]{2,1,0:T(8,128)(2,1)S(1)} collective-permute-done((bf16[4,112,512]{2,1,0:T(8,128)(2,1)S(1)}, bf16[4,112,512]{2,1,0:T(8,128)(2,1)S(1)}, u32[]{:S(2)}, u32[]{:S(2)}) %collective-permute-start.5) | collective-permute-done | bytes 458784 | tf_op jit(solution)/shard_map/ppermute | solution.py:285
  55.7 3.9 %collective-permute-done.4 = bf16[4,112,512]{2,1,0:T(8,128)(2,1)S(1)} collective-permute-done((bf16[4,112,512]{2,1,0:T(8,128)(2,1)S(1)}, bf16[4,112,512]{2,1,0:T(8,128)(2,1)S(1)}, u32[]{:S(2)}, u32[]{:S(2)}) %collective-permute-start.4) | collective-permute-done | bytes 458784 | tf_op jit(solution)/shard_map/ppermute | solution.py:285
  59.6 3.6 %collective-permute-start.16 = (bf16[256,512]{1,0:T(8,128)(2,1)S(1)}, bf16[256,512]{1,0:T(8,128)(2,1)S(1)}, u32[]{:S(2)}, u32[]{:S(2)}) collective-permute-start(bf16[256,512]{1,0:T(8,128)(2,1)S(1)} %copy-done.12), channel_id=1, source_target_pairs={{64,0},{128,64},{192,128},{0,192},{65,1},{129,65},{193,129},{1,193... | collective-permute-start | bytes 786440 | tf_op jit(solution)/shard_map/ppermute | solution.py:285
  63.1 1.7 collective-permute-start.2
  64.8 4.0 %collective-permute-start.3 = (bf16[512,896]{1,0:T(8,128)(2,1)}, bf16[512,896]{1,0:T(8,128)(2,1)}, u32[]{:S(2)}, u32[]{:S(2)}) collective-permute-start(bf16[512,896]{1,0:T(8,128)(2,1)} %collective-permute-done.1.refs_2_), channel_id=1, source_target_pairs={{0,28},{4,0},{8,4},{12,8},{16,12},{20,16},{24,20},{28,24},{1,29},{... | collective-permute-start | bytes 2752520 | tf_op jit(solution)/shard_map/ppermute | solution.py:300
  68.9 1.2 pad_maximum_fusion.refs_5_.refs_2_
  70.1 1.1 collective-permute-start.7
  72.8 8.6 %all-to-all-start = ((f32[32,8,128]{2,1,0:T(8,128)}), f32[32,8,128]{2,1,0:T(8,128)S(1)}, u32[]{:S(2)}, u32[]{:S(2)}) async-start(f32[32,8,128]{2,1,0:T(8,128)} %bitcast.5), calls=%async_computation | async-start | bytes 262144 | tf_op jit(solution)/shard_map/all_to_all | solution.py:357
  81.5 7.5 %collective-permute-done.2.refs_3_ = bf16[512,896]{1,0:T(8,128)(2,1)} collective-permute-done((bf16[512,896]{1,0:T(8,128)(2,1)}, bf16[512,896]{1,0:T(8,128)(2,1)}, u32[]{:S(2)}, u32[]{:S(2)}) %collective-permute-start.2) | collective-permute-done | bytes 917536 | tf_op jit(solution)/shard_map/ppermute | solution.py:299
  89.4 3.6 %collective-permute-start.10 = (bf16[512,896]{1,0:T(8,128)(2,1)}, bf16[512,896]{1,0:T(8,128)(2,1)}, u32[]{:S(2)}, u32[]{:S(2)}) collective-permute-start(bf16[512,896]{1,0:T(8,128)(2,1)} %collective-permute-done.3.refs_4_), channel_id=1, source_target_pairs={{0,28},{4,0},{8,4},{12,8},{16,12},{20,16},{24,20},{28,24},{1,29},{... | collective-permute-start | bytes 2752520 | tf_op jit(solution)/shard_map/ppermute | solution.py:300
  94.0 1.1 broadcast_in_dim.106
  95.0 1.3 reshape.146.scale_ref
  96.4 1.1 reshape.148
  97.4 5.3 %codes.1 = f32[160,512]{1,0:T(8,128)} custom-call(s32[2]{0:T(128)} %pad_add_fusion.here_ref.core_ref, bf16[8,160,2048]{2,1,0:T(8,128)(2,1)} %hidden_ref.3, bf16[4,256,512]{2,1,0:T(8,128)(2,1)} %copy-done.2, bf16[4,256,512]{2,1,0:T(8,128)(2,1)} %collective-permute-done.19.theirs_ref), custom_call_target="tpu_custom_call" | custom-call | flops 671088640 | bytes 7340032 | tf_op jit(solution)/shard_map/codes/pallas_call | solution.py:76
  102.7 1.3 convolution_convert_fusion
  105.1 3.5 %all-to-all-start.5 = ((bf16[4,256,512]{2,1,0:T(8,128)(2,1)}), bf16[4,256,512]{2,1,0:T(8,128)(2,1)S(1)}, u32[]{:S(2)}, u32[]{:S(2)}) async-start(bf16[4,256,512]{2,1,0:T(8,128)(2,1)} %broadcast_in_dim.108), calls=%async_computation.5 | async-start | bytes 2097152 | tf_op jit(solution)/shard_map/all_to_all | solution.py:390
  109.7 1.4 copy.65
  111.8 1.1 slice.50
  113.9 1.1 slice.51
  114.9 1.8 collective-permute-start.11
  116.7 17.6 %back.3 = (f32[4,160,512]{2,1,0:T(8,128)}, bf16[4,8,160,896]{3,2,1,0:T(8,128)(2,1)}) custom-call(s32[2]{0:T(128)} %pad_add_fusion.here_ref.core_ref, s32[4,16,128]{2,1,0:T(8,128)} %copy.70.index_ref, bf16[512,896]{1,0:T(8,128)(2,1)} %bitcast.57, bf16[512,896]{1,0:T(8,128)(2,1)} %collective-permute-done.refs_1_, ...), custom_call_target="tpu_custom_call" | custom-call | flops 4697620480 | bytes 18743296 | tf_op jit(solution)/shard_map/back/pallas_call | solution.py:206
  134.3 8.5 %back.4 = (f32[4,96,512]{2,1,0:T(8,128)}, bf16[4,8,64,896]{3,2,1,0:T(8,128)(2,1)}) custom-call(s32[2]{0:T(128)} %pad_add_fusion.here_ref.core_ref, s32[4,16,128]{2,1,0:T(8,128)} %copy.70.index_ref, bf16[512,896]{1,0:T(8,128)(2,1)} %collective-permute-done.8.refs_0_, bf16[512,896]{1,0:T(8,128)(2,1)} %collective-permute-done.10.refs_1_, ...), custom_call_target="tpu_custom_call" | custom-call | flops 1879048192 | bytes 9699328 | tf_op jit(solution)/shard_map/back/pallas_call | solution.py:206
  143.7 5.1 %back.5 = (f32[4,96,512]{2,1,0:T(8,128)}, bf16[4,8,32,896]{3,2,1,0:T(8,128)(2,1)}) custom-call(s32[2]{0:T(128)} %pad_add_fusion.here_ref.core_ref, s32[4,16,128]{2,1,0:T(8,128)} %copy.70.index_ref, bf16[256,896]{1,0:T(8,128)(2,1)} %copy-done.10, bf16[256,896]{1,0:T(8,128)(2,1)} %copy-done.11, ...), custom_call_target="tpu_custom_call", output_to_operand_aliasing={{0}: (6, {})} | custom-call | flops 939524096 | bytes 6684672 | tf_op jit(solution)/shard_map/back/pallas_call | solution.py:206
  149.9 16.1 %grad_out.1 = (f32[4,4,112,512]{3,2,1,0:T(8,128)}, f32[4,4,112,512]{3,2,1,0:T(8,128)}) custom-call(s32[2]{0:T(128)} %pad_add_fusion.here_ref.core_ref, bf16[4,8,160,896]{3,2,1,0:T(8,128)(2,1)} %get-tuple-element.17.refs_0_, bf16[4,8,64,896]{3,2,1,0:T(8,128)(2,1)} %get-tuple-element.18.refs_1_, bf16[4,8,32,896]{3,2,1,0:T(8,128)(2,1)} %get-tuple-element.19.refs_2_, ...), custom_call_target="tpu_custom_call" | custom-call | flops 1879048192 | bytes 22020096 | tf_op jit(solution)/shard_map/grad_out/pallas_call | solution.py:256
  166.0 3.2 %collective-permute-start.20 = (f32[4,4,112,512]{3,2,1,0:T(8,128)}, f32[4,4,112,512]{3,2,1,0:T(8,128)}, u32[]{:S(2)}, u32[]{:S(2)}) collective-permute-start(f32[4,4,112,512]{3,2,1,0:T(8,128)} %get-tuple-element.21), channel_id=1, source_target_pairs={{0,32},{32,0},{1,33},{33,1},{2,34},{34,2},{3,35},{35,3},{4,36},{36... | collective-permute-start | bytes 11010056 | tf_op jit(solution)/shard_map/ppermute | solution.py:406
  169.2 22.1 %all_to_all.50.refs_0_ = f32[4,160,512]{2,1,0:T(8,128)} all-to-all(f32[4,160,512]{2,1,0:T(8,128)S(1)} %copy-done.6), channel_id=1, replica_groups=mesh['y'=4,'c'=2,'z'=8,'x'=4] {'x'}, dimensions={0} | all-to-all | bytes 2621440 | tf_op jit(solution)/shard_map/all_to_all | solution.py:404
  191.2 3.5 %all-to-all-start.4 = ((f32[4,96,512]{2,1,0:T(8,128)}), f32[4,96,512]{2,1,0:T(8,128)S(1)}, u32[]{:S(2)}, u32[]{:S(2)}) async-start(f32[4,96,512]{2,1,0:T(8,128)} %get-tuple-element.14), calls=%async_computation.4 | async-start | bytes 1572864 | tf_op jit(solution)/shard_map/all_to_all | solution.py:404
  195.5 10.5 %all-to-all-done.4.refs_1_ = f32[4,96,512]{2,1,0:T(8,128)S(1)} async-done(((f32[4,96,512]{2,1,0:T(8,128)}), f32[4,96,512]{2,1,0:T(8,128)S(1)}, u32[]{:S(2)}, u32[]{:S(2)}) %all-to-all-start.4) | async-done | bytes 786464 | tf_op jit(solution)/shard_map/all_to_all | solution.py:404
  206.8 7.8 %grad_in.1 = (f32[4,256,512]{2,1,0:T(8,128)}, f32[4,256,512]{2,1,0:T(8,128)}) custom-call(s32[2]{0:T(128)} %pad_add_fusion.here_ref.core_ref, bf16[8,160,2048]{2,1,0:T(8,128)(2,1)} %hidden_ref.3, bf16[160,256]{1,0:T(8,128)(2,1)} %fusion.17.pick_ref, f32[160,512]{1,0:T(8,128)} %copy-done.4, f32[4,160,512]{2,1,0:T(8,128)} %all_to_all.50.refs_0_, ...), custom_call_target="tpu_custom_call" | custom-call | flops 1342177280 | bytes 9437184 | tf_op jit(solution)/shard_map/grad_in/pallas_call | solution.py:136
  214.6 2.0 collective-permute-start.12
  216.7 5.0 %add_convert_fusion = bf16[4,4,112,512]{3,2,1,0:T(8,128)(2,1)} fusion(f32[4,4,112,512]{3,2,1,0:T(8,128)} %get-tuple-element.20, f32[4,4,112,512]{3,2,1,0:T(8,128)} %collective-permute-done.20), kind=kLoop, calls=%fused_computation.1 | loop fusion | flops 1835008 | bytes 9175040 | tf_op jit(solution)/shard_map/convert_element_type | solution.py:409
  221.7 3.9 %all-to-all-start.6 = ((bf16[16,112,512]{2,1,0:T(8,128)(2,1)}), bf16[16,112,512]{2,1,0:T(8,128)(2,1)S(1)}, u32[]{:S(2)}, u32[]{:S(2)}) async-start(bf16[16,112,512]{2,1,0:T(8,128)(2,1)} %bitcast.49), calls=%async_computation.6 | async-start | bytes 3670016 | tf_op jit(solution)/shard_map/all_to_all | solution.py:411
  225.7 2.1 fusion.14
  227.8 2.4 collective-permute-start.15
  231.3 21.7 %collective-permute-done.15 = bf16[256,512]{1,0:T(8,128)(2,1)S(1)} collective-permute-done((bf16[256,512]{1,0:T(8,128)(2,1)S(1)}, bf16[256,512]{1,0:T(8,128)(2,1)S(1)}, u32[]{:S(2)}, u32[]{:S(2)}) %collective-permute-start.15) | collective-permute-done | bytes 262176 | tf_op jit(solution)/shard_map/ppermute | solution.py:417
  253.0 7.1 %collective-permute-done.13 = bf16[256,512]{1,0:T(8,128)(2,1)S(1)} collective-permute-done((bf16[256,512]{1,0:T(8,128)(2,1)S(1)}, bf16[256,512]{1,0:T(8,128)(2,1)S(1)}, u32[]{:S(2)}, u32[]{:S(2)}) %collective-permute-start.13) | collective-permute-done | bytes 262176 | tf_op jit(solution)/shard_map/ppermute | solution.py:417
  260.0 2.2 fusion.13
  262.2 1.2 convert_reduce_fusion
  (98 shorter events, 15.1 us)
Async XLA Ops:
  0.6 1.7 copy-start.7
  0.6 2.3 copy-start.16
  0.7 2.3 copy-start.13
  0.7 3.6 %copy-start.17 = (s32[128]{0:T(128)S(1)}, s32[128]{0:T(128)}, u32[]{:S(2)}) copy-start(s32[128]{0:T(128)} %param.12) | copy-start | bytes 1540
  23.4 10.0 %copy-start.14 = (s32[128,8]{0,1:T(8,128)S(1)}, s32[128,8]{0,1:T(8,128)}, u32[]{:S(2)}) copy-start(s32[128,8]{0,1:T(8,128)} %param.10) | copy-start | bytes 12292
  23.4 15.8 %copy-start.15 = (f32[128,8]{0,1:T(8,128)S(1)}, f32[128,8]{0,1:T(8,128)}, u32[]{:S(2)}) copy-start(f32[128,8]{0,1:T(8,128)} %param.11) | copy-start | bytes 12292
  23.4 21.0 %copy-start.12 = (bf16[256,512]{1,0:T(8,128)(2,1)S(1)}, bf16[256,512]{1,0:T(8,128)(2,1)}, u32[]{:S(2)}) copy-start(bf16[256,512]{1,0:T(8,128)(2,1)} %param.18) | copy-start | bytes 786436
  23.4 10.3 %all-to-all-start.2 = ((bf16[4,112,512]{2,1,0:T(8,128)(2,1)}), bf16[4,112,512]{2,1,0:T(8,128)(2,1)S(1)}, u32[]{:S(2)}, u32[]{:S(2)}) async-start(bf16[4,112,512]{2,1,0:T(8,128)(2,1)} %bitcast.13), calls=%async_computation.2 | async-start | bytes 917504 | tf_op jit(solution)/shard_map/all_to_all | solution.py:372
  27.6 41.2 %copy-start.8 = (bf16[4,128,896]{2,1,0:T(8,128)(2,1)}, bf16[4,128,896]{2,1,0:T(8,128)(2,1)S(1)}, u32[]{:S(2)}) copy-start(bf16[4,128,896]{2,1,0:T(8,128)(2,1)S(1)} %copy.69) | copy-start | bytes 2752516
  27.6 35.5 %collective-permute-start = (bf16[512,896]{1,0:T(8,128)(2,1)S(1)}, bf16[512,896]{1,0:T(8,128)(2,1)}, u32[]{:S(2)}, u32[]{:S(2)}) collective-permute-start(bf16[512,896]{1,0:T(8,128)(2,1)S(1)} %bitcast.55), channel_id=1, source_target_pairs={{0,4},{4,8},{8,12},{12,16},{16,20},{20,24},{24,28},{28,0},{1,5},{5... | collective-permute-start | bytes 2752520 | tf_op jit(solution)/shard_map/ppermute | solution.py:299
  29.4 35.4 %collective-permute-start.1 = (bf16[512,896]{1,0:T(8,128)(2,1)S(1)}, bf16[512,896]{1,0:T(8,128)(2,1)}, u32[]{:S(2)}, u32[]{:S(2)}) collective-permute-start(bf16[512,896]{1,0:T(8,128)(2,1)S(1)} %bitcast.56), channel_id=1, source_target_pairs={{0,28},{4,0},{8,4},{12,8},{16,12},{20,16},{24,20},{28,24},{1,29},{... | collective-permute-start | bytes 2752520 | tf_op jit(solution)/shard_map/ppermute | solution.py:300
  33.7 10.7 %collective-permute-start.6 = (bf16[4,112,512]{2,1,0:T(8,128)(2,1)S(1)}, bf16[4,112,512]{2,1,0:T(8,128)(2,1)S(1)}, u32[]{:S(2)}, u32[]{:S(2)}) collective-permute-start(bf16[4,112,512]{2,1,0:T(8,128)(2,1)S(1)} %all-to-all-done.2), channel_id=1, source_target_pairs={{192,0},{0,64},{64,128},{128,192},{193,1},{1,65},{65,129},{129,193... | collective-permute-start | bytes 1376264 | tf_op jit(solution)/shard_map/ppermute | solution.py:285
  35.1 20.1 %collective-permute-start.5 = (bf16[4,112,512]{2,1,0:T(8,128)(2,1)S(1)}, bf16[4,112,512]{2,1,0:T(8,128)(2,1)S(1)}, u32[]{:S(2)}, u32[]{:S(2)}) collective-permute-start(bf16[4,112,512]{2,1,0:T(8,128)(2,1)S(1)} %all-to-all-done.2), channel_id=1, source_target_pairs={{128,0},{192,64},{0,128},{64,192},{129,1},{193,65},{1,129},{65,193... | collective-permute-start | bytes 1376264 | tf_op jit(solution)/shard_map/ppermute | solution.py:285
  37.7 21.9 %collective-permute-start.4 = (bf16[4,112,512]{2,1,0:T(8,128)(2,1)S(1)}, bf16[4,112,512]{2,1,0:T(8,128)(2,1)S(1)}, u32[]{:S(2)}, u32[]{:S(2)}) collective-permute-start(bf16[4,112,512]{2,1,0:T(8,128)(2,1)S(1)} %all-to-all-done.2), channel_id=1, source_target_pairs={{64,0},{128,64},{192,128},{0,192},{65,1},{129,65},{193,129},{1,193... | collective-permute-start | bytes 1376264 | tf_op jit(solution)/shard_map/ppermute | solution.py:285
  44.4 25.8 %collective-permute-start.18 = (bf16[256,512]{1,0:T(8,128)(2,1)S(1)}, bf16[256,512]{1,0:T(8,128)(2,1)S(1)}, u32[]{:S(2)}, u32[]{:S(2)}) collective-permute-start(bf16[256,512]{1,0:T(8,128)(2,1)S(1)} %copy-done.12), channel_id=1, source_target_pairs={{192,0},{0,64},{64,128},{128,192},{193,1},{1,65},{65,129},{129,193... | collective-permute-start | bytes 786440 | tf_op jit(solution)/shard_map/ppermute | solution.py:285
  55.2 16.1 %collective-permute-start.17 = (bf16[256,512]{1,0:T(8,128)(2,1)S(1)}, bf16[256,512]{1,0:T(8,128)(2,1)S(1)}, u32[]{:S(2)}, u32[]{:S(2)}) collective-permute-start(bf16[256,512]{1,0:T(8,128)(2,1)S(1)} %copy-done.12), channel_id=1, source_target_pairs={{128,0},{192,64},{0,128},{64,192},{129,1},{193,65},{1,129},{65,193... | collective-permute-start | bytes 786440 | tf_op jit(solution)/shard_map/ppermute | solution.py:285
  59.6 9.3 %copy-start.9 = (bf16[4,112,512]{2,1,0:T(8,128)(2,1)}, bf16[4,112,512]{2,1,0:T(8,128)(2,1)S(1)}, u32[]{:S(2)}) copy-start(bf16[4,112,512]{2,1,0:T(8,128)(2,1)S(1)} %collective-permute-done.4) | copy-start | bytes 1376260
  59.6 11.7 %collective-permute-start.16 = (bf16[256,512]{1,0:T(8,128)(2,1)S(1)}, bf16[256,512]{1,0:T(8,128)(2,1)S(1)}, u32[]{:S(2)}, u32[]{:S(2)}) collective-permute-start(bf16[256,512]{1,0:T(8,128)(2,1)S(1)} %copy-done.12), channel_id=1, source_target_pairs={{64,0},{128,64},{192,128},{0,192},{65,1},{129,65},{193,129},{1,193... | collective-permute-start | bytes 786440 | tf_op jit(solution)/shard_map/ppermute | solution.py:285
  63.1 25.9 %collective-permute-start.2 = (bf16[512,896]{1,0:T(8,128)(2,1)}, bf16[512,896]{1,0:T(8,128)(2,1)}, u32[]{:S(2)}, u32[]{:S(2)}) collective-permute-start(bf16[512,896]{1,0:T(8,128)(2,1)} %collective-permute-done.refs_1_), channel_id=1, source_target_pairs={{0,4},{4,8},{8,12},{12,16},{16,20},{20,24},{24,28},{28,0},{1,5},{5... | collective-permute-start | bytes 2752520 | tf_op jit(solution)/shard_map/ppermute | solution.py:299
  64.8 24.6 %collective-permute-start.3 = (bf16[512,896]{1,0:T(8,128)(2,1)}, bf16[512,896]{1,0:T(8,128)(2,1)}, u32[]{:S(2)}, u32[]{:S(2)}) collective-permute-start(bf16[512,896]{1,0:T(8,128)(2,1)} %collective-permute-done.1.refs_2_), channel_id=1, source_target_pairs={{0,28},{4,0},{8,4},{12,8},{16,12},{20,16},{24,20},{28,24},{1,29},{... | collective-permute-start | bytes 2752520 | tf_op jit(solution)/shard_map/ppermute | solution.py:300
  70.1 2.7 %copy-start = (bf16[4,4,112,512]{3,2,1,0:T(8,128)(2,1)}, bf16[4,4,112,512]{3,2,1,0:T(8,128)(2,1)S(1)}, u32[]{:S(2)}) copy-start(bf16[4,4,112,512]{3,2,1,0:T(8,128)(2,1)S(1)} %pad_maximum_fusion.refs_5_.refs_2_) | copy-start | bytes 5505028
  70.1 46.6 %collective-permute-start.7 = (bf16[4,4,112,512]{3,2,1,0:T(8,128)(2,1)S(1)}, bf16[4,4,112,512]{3,2,1,0:T(8,128)(2,1)}, u32[]{:S(2)}, u32[]{:S(2)}) collective-permute-start(bf16[4,4,112,512]{3,2,1,0:T(8,128)(2,1)S(1)} %pad_maximum_fusion.refs_5_.refs_2_), channel_id=1, source_target_pairs={{0,32},{32,0},{1,33},{33,1},{2,34},{34,2},{3,35},{35,3},{4,36},{36... | collective-permute-start | bytes 5505032 | tf_op jit(solution)/shard_map/ppermute | solution.py:287
  71.4 24.9 %copy-start.2 = (bf16[4,256,512]{2,1,0:T(8,128)(2,1)}, bf16[4,256,512]{2,1,0:T(8,128)(2,1)S(1)}, u32[]{:S(2)}) copy-start(bf16[4,256,512]{2,1,0:T(8,128)(2,1)S(1)} %pad_maximum_fusion.1.mine_ref) | copy-start | bytes 3145732
  71.4 26.0 %collective-permute-start.19 = (bf16[4,256,512]{2,1,0:T(8,128)(2,1)S(1)}, bf16[4,256,512]{2,1,0:T(8,128)(2,1)}, u32[]{:S(2)}, u32[]{:S(2)}) collective-permute-start(bf16[4,256,512]{2,1,0:T(8,128)(2,1)S(1)} %pad_maximum_fusion.1.mine_ref), channel_id=1, source_target_pairs={{0,32},{32,0},{1,33},{33,1},{2,34},{34,2},{3,35},{35,3},{4,36},{36... | collective-permute-start | bytes 3145736 | tf_op jit(solution)/shard_map/ppermute | solution.py:287
  72.8 20.8 %all-to-all-start = ((f32[32,8,128]{2,1,0:T(8,128)}), f32[32,8,128]{2,1,0:T(8,128)S(1)}, u32[]{:S(2)}, u32[]{:S(2)}) async-start(f32[32,8,128]{2,1,0:T(8,128)} %bitcast.5), calls=%async_computation | async-start | bytes 262144 | tf_op jit(solution)/shard_map/all_to_all | solution.py:357
  89.0 22.7 %collective-permute-start.8 = (bf16[512,896]{1,0:T(8,128)(2,1)}, bf16[512,896]{1,0:T(8,128)(2,1)}, u32[]{:S(2)}, u32[]{:S(2)}) collective-permute-start(bf16[512,896]{1,0:T(8,128)(2,1)} %collective-permute-done.2.refs_3_), channel_id=1, source_target_pairs={{0,4},{4,8},{8,12},{12,16},{16,20},{20,24},{24,28},{28,0},{1,5},{5... | collective-permute-start | bytes 2752520 | tf_op jit(solution)/shard_map/ppermute | solution.py:299
  89.4 24.5 %collective-permute-start.10 = (bf16[512,896]{1,0:T(8,128)(2,1)}, bf16[512,896]{1,0:T(8,128)(2,1)}, u32[]{:S(2)}, u32[]{:S(2)}) collective-permute-start(bf16[512,896]{1,0:T(8,128)(2,1)} %collective-permute-done.3.refs_4_), channel_id=1, source_target_pairs={{0,28},{4,0},{8,4},{12,8},{16,12},{20,16},{24,20},{28,24},{1,29},{... | collective-permute-start | bytes 2752520 | tf_op jit(solution)/shard_map/ppermute | solution.py:300
  96.3 6.4 %copy-start.4 = (f32[160,512]{1,0:T(8,128)}, f32[160,512]{1,0:T(8,128)S(1)}, u32[]{:S(2)}) copy-start(f32[160,512]{1,0:T(8,128)S(1)} %reshape.146.scale_ref) | copy-start | bytes 983044
  104.1 4.6 %copy-start.5 = (s32[16,2,8,4,8]{4,3,2,1,0:T(4,128)S(1)}, s32[16,2,8,4,8]{4,3,2,1,0:T(4,128)}, u32[]{:S(2)}) copy-start(s32[16,2,8,4,8]{4,3,2,1,0:T(4,128)} %reshape.148) | copy-start | bytes 98308
  105.1 43.8 %all-to-all-start.5 = ((bf16[4,256,512]{2,1,0:T(8,128)(2,1)}), bf16[4,256,512]{2,1,0:T(8,128)(2,1)S(1)}, u32[]{:S(2)}, u32[]{:S(2)}) async-start(bf16[4,256,512]{2,1,0:T(8,128)(2,1)} %broadcast_in_dim.108), calls=%async_computation.5 | async-start | bytes 2097152 | tf_op jit(solution)/shard_map/all_to_all | solution.py:390
  112.8 30.0 %collective-permute-start.9 = (bf16[256,896]{1,0:T(8,128)(2,1)S(1)}, bf16[256,896]{1,0:T(8,128)(2,1)S(1)}, u32[]{:S(2)}, u32[]{:S(2)}) collective-permute-start(bf16[256,896]{1,0:T(8,128)(2,1)S(1)} %slice.50), channel_id=1, source_target_pairs={{0,4},{4,8},{8,12},{12,16},{16,20},{20,24},{24,28},{28,0},{1,5},{5... | collective-permute-start | bytes 1376264 | tf_op jit(solution)/shard_map/ppermute | solution.py:307
  114.9 27.9 %collective-permute-start.11 = (bf16[256,896]{1,0:T(8,128)(2,1)S(1)}, bf16[256,896]{1,0:T(8,128)(2,1)S(1)}, u32[]{:S(2)}, u32[]{:S(2)}) collective-permute-start(bf16[256,896]{1,0:T(8,128)(2,1)S(1)} %slice.51), channel_id=1, source_target_pairs={{0,28},{4,0},{8,4},{12,8},{16,12},{20,16},{24,20},{28,24},{1,29},{... | collective-permute-start | bytes 1376264 | tf_op jit(solution)/shard_map/ppermute | solution.py:308
  142.8 0.8 copy-start.10
  142.8 0.9 copy-start.11
  148.9 1.0 copy-start.1
  149.9 19.3 %copy-start.6 = (f32[4,160,512]{2,1,0:T(8,128)S(1)}, f32[4,160,512]{2,1,0:T(8,128)}, u32[]{:S(2)}) copy-start(f32[4,160,512]{2,1,0:T(8,128)} %get-tuple-element.12) | copy-start | bytes 3932164
  166.0 50.7 %collective-permute-start.20 = (f32[4,4,112,512]{3,2,1,0:T(8,128)}, f32[4,4,112,512]{3,2,1,0:T(8,128)}, u32[]{:S(2)}, u32[]{:S(2)}) collective-permute-start(f32[4,4,112,512]{3,2,1,0:T(8,128)} %get-tuple-element.21), channel_id=1, source_target_pairs={{0,32},{32,0},{1,33},{33,1},{2,34},{34,2},{3,35},{35,3},{4,36},{36... | collective-permute-start | bytes 11010056 | tf_op jit(solution)/shard_map/ppermute | solution.py:406
  191.2 14.7 %all-to-all-start.4 = ((f32[4,96,512]{2,1,0:T(8,128)}), f32[4,96,512]{2,1,0:T(8,128)S(1)}, u32[]{:S(2)}, u32[]{:S(2)}) async-start(f32[4,96,512]{2,1,0:T(8,128)} %get-tuple-element.14), calls=%async_computation.4 | async-start | bytes 1572864 | tf_op jit(solution)/shard_map/all_to_all | solution.py:404
  205.9 0.9 copy-start.3
  214.6 11.0 %collective-permute-start.12 = (f32[4,256,512]{2,1,0:T(8,128)}, f32[4,256,512]{2,1,0:T(8,128)}, u32[]{:S(2)}, u32[]{:S(2)}) collective-permute-start(f32[4,256,512]{2,1,0:T(8,128)} %get-tuple-element.16), channel_id=1, source_target_pairs={{0,32},{32,0},{1,33},{33,1},{2,34},{34,2},{3,35},{35,3},{4,36},{36... | collective-permute-start | bytes 6291464 | tf_op jit(solution)/shard_map/ppermute | solution.py:408
  221.7 40.5 %all-to-all-start.6 = ((bf16[16,112,512]{2,1,0:T(8,128)(2,1)}), bf16[16,112,512]{2,1,0:T(8,128)(2,1)S(1)}, u32[]{:S(2)}, u32[]{:S(2)}) async-start(bf16[16,112,512]{2,1,0:T(8,128)(2,1)} %bitcast.49), calls=%async_computation.6 | async-start | bytes 3670016 | tf_op jit(solution)/shard_map/all_to_all | solution.py:411
  227.8 25.2 %collective-permute-start.15 = (bf16[256,512]{1,0:T(8,128)(2,1)S(1)}, bf16[256,512]{1,0:T(8,128)(2,1)S(1)}, u32[]{:S(2)}, u32[]{:S(2)}) collective-permute-start(bf16[256,512]{1,0:T(8,128)(2,1)S(1)} %get-tuple-element.25), channel_id=1, source_target_pairs={{0,192},{64,0},{128,64},{192,128},{1,193},{65,1},{129,65},{193,129... | collective-permute-start | bytes 786440 | tf_op jit(solution)/shard_map/ppermute | solution.py:417
  230.1 22.8 %collective-permute-start.14 = (bf16[256,512]{1,0:T(8,128)(2,1)S(1)}, bf16[256,512]{1,0:T(8,128)(2,1)S(1)}, u32[]{:S(2)}, u32[]{:S(2)}) collective-permute-start(bf16[256,512]{1,0:T(8,128)(2,1)S(1)} %get-tuple-element.26), channel_id=1, source_target_pairs={{0,128},{64,192},{128,0},{192,64},{1,129},{65,193},{129,1},{193,65... | collective-permute-start | bytes 786440 | tf_op jit(solution)/shard_map/ppermute | solution.py:417
  230.7 29.4 %collective-permute-start.13 = (bf16[256,512]{1,0:T(8,128)(2,1)S(1)}, bf16[256,512]{1,0:T(8,128)(2,1)S(1)}, u32[]{:S(2)}, u32[]{:S(2)}) collective-permute-start(bf16[256,512]{1,0:T(8,128)(2,1)S(1)} %get-tuple-element.24), channel_id=1, source_target_pairs={{0,64},{64,128},{128,192},{192,0},{1,65},{65,129},{129,193},{193,1... | collective-permute-start | bytes 786440 | tf_op jit(solution)/shard_map/ppermute | solution.py:417
